TPU v7x, 32 devices: a whole 2x2x4 slice. The times are simulated.
32 devices in a mesh: frames: 4 (over y, x), tiles: 8 (over z, core).
Axes of the slice: x: 2, y: 2, z: 4, core: 2. Of those that a mesh axis runs over, the one named last changes fastest.
Arguments:
- features: bfloat16 [16, 64, 480, 128], P('frames', 'tiles'), may hold values from -6 to 6
- w_conv: bfloat16 [3, 3, 128, 128], replicated, may hold values from -0.1875 to 0.1875
- query_feats: bfloat16 [4096, 128], P(('frames', 'tiles')), may hold values from -6 to 6
- offset_rows: int32 [16, 32], P('frames'), may hold values from 0 to 7
- offset_cols: int32 [16, 32], P('frames'), may hold values from 0 to 471
- owners: int32 [32, 1], replicated, may hold values from 0 to 7; in each aligned block of 32 rows (0 to 31, 32 to 63, ...) at most 12 rows name the same one
- start_frames: int32 [4096], P(('frames', 'tiles')), may hold values from 0 to 15
- w_corr: bfloat16 [81, 384], replicated, may hold values from -0.625 to 0.625
- w_feat: bfloat16 [128, 384], replicated, may hold values from -0.5 to 0.5
- time_embed: float32 [16, 384], replicated, may hold values from -3 to 3
- gain_attn: float32 [384], replicated, may hold values from 0.5 to 1.5
- w_qkv: bfloat16 [384, 1152], replicated, may hold values from -1.0716518 to 1.0716518
- w_attn_out: bfloat16 [384, 384], replicated, may hold values from -0.3125 to 0.3125
- gain_mlp: float32 [384], replicated, may hold values from 0.5 to 1.5
- w_up: bfloat16 [384, 1536], replicated, may hold values from -0.3125 to 0.3125
- w_down: bfloat16 [1536, 384], replicated, may hold values from -0.15625 to 0.15625
Outputs:
- refined: bfloat16 [4096, 16, 384], P(('frames', 'tiles'))
Inputs may be any that keep to these rules, and one draw needn't show every extreme that they name: `owners`: no tile owns more than 12 query blocks; some tile owns exactly 12; every tile owns at least one.
All inputs are finite; a program needn't handle non-finite values.
Results may differ from a plain program's by a relative error of at most 0.0066.
Values may be sent and summed in bfloat16 or wider, within the bound.
A program may use at most 192 MiB of HBM per device.

v0:
```python
import functools
import math

import jax
import jax.numpy as jnp
from jax import lax
from jax.experimental import pallas as pl
from jax.experimental.pallas import tpu as pltpu
from jax.sharding import PartitionSpec as P

HEADS = 8
WIN = 9
QBLK = 128
CELLS = 88
REACH = WIN // 2
GROUP = 8
F32 = jnp.float32
BF16 = jnp.bfloat16
MESH = pl.DeviceIdType.MESH


def reversed_bits(value, bits):
    out = value * 0
    for bit in range(bits):
        out = out + ((value // 2**bit) % 2) * 2 ** (bits - 1 - bit)
    return out


def window_kernel(
    n_tiles, n_frames, owners, row_off, col_off, feat, w_conv, out, w_cat, padded, conv, win, parts, *scratch
):
    levels = n_tiles.bit_length() - 1
    sums, lands = scratch[:levels], scratch[levels : 2 * levels]
    feat_sem, send_sem, recv_sem, out_send, out_recv = scratch[2 * levels :]
    tile, group = lax.axis_index("tiles"), lax.axis_index("frames")
    frame_dev, rows, cols, chans = feat.shape
    blocks = owners.shape[0]
    per_group = blocks // n_frames
    blk_dev = out.shape[1]

    def fetch(frame):
        return pltpu.make_async_copy(feat.at[frame], padded.at[frame, pl.ds(2, rows)], feat_sem.at[frame])

    for frame in range(frame_dev):
        fetch(frame).start()
    partners = []
    for level in range(levels):
        bit = (tile // 2**level) % 2
        partners.append((group, tile + (1 - 2 * bit) * 2**level))
    peers = [((group + step) % n_frames, tile) for step in range(1, n_frames)]
    barrier = pltpu.get_barrier_semaphore()
    for device in partners + peers:
        pl.semaphore_signal(barrier, inc=1, device_id=device, device_id_type=MESH)

    blank = jnp.zeros((2, cols, chans), BF16)
    for frame in range(frame_dev):
        padded[frame, 0:2] = blank
        padded[frame, rows + 2 : rows + 4] = blank
    win[...] = jnp.zeros_like(win)
    for y in range(WIN):
        conv[y] = jnp.zeros(conv.shape[1:], F32)
        conv[WIN + rows + 2 + y] = jnp.zeros(conv.shape[1:], F32)
    conv[WIN : WIN + rows + 2, cols:] = jnp.zeros((rows + 2, conv.shape[1] - cols, chans), F32)
    for a in range(3):
        for b in range(3):
            w_cat[a * chans : (a + 1) * chans, b * chans : (b + 1) * chans] = w_conv[a, b]

    def halving(level, frame):
        source = parts if level == 0 else sums[level - 1]
        count = n_tiles >> (level + 1)
        bit = (tile // 2**level) % 2
        copy = pltpu.make_async_remote_copy(
            src_ref=source.at[frame, pl.ds((1 - bit) * count, count)],
            dst_ref=lands[level].at[frame],
            send_sem=send_sem.at[level, frame],
            recv_sem=recv_sem.at[level, frame],
            device_id=partners[level],
            device_id_type=MESH,
        )
        return copy, source, bit * count, count

    def handing(step, frame, giver):
        return pltpu.make_async_remote_copy(
            src_ref=sums[levels - 1].at[frame, 0, pl.ds(peers[step][0] * blk_dev, blk_dev)],
            dst_ref=out.at[giver * frame_dev + frame],
            send_sem=out_send.at[step, frame],
            recv_sem=out_recv.at[step, frame],
            device_id=peers[step],
            device_id_type=MESH,
        )

    def convolve(frame):
        fetch(frame).wait()

        def conv_rows(pair, carry):
            for half in range(2):
                y = 2 * pair + half
                wide = jnp.concatenate([padded[frame, y], padded[frame, y + 1], padded[frame, y + 2]], axis=-1)
                sums_at = jnp.dot(wide, w_cat[...], preferred_element_type=F32)
                edge = jnp.zeros((1, chans), F32)
                left = jnp.concatenate([edge, sums_at[: cols - 1, :chans]], axis=0)
                right = jnp.concatenate([sums_at[1:, 2 * chans :], edge], axis=0)
                conv[WIN + y, :cols] = left + sums_at[:, chans : 2 * chans] + right
            return carry

        lax.fori_loop(0, (rows + 2) // 2, conv_rows, 0)

        @pl.when(tile == 0)
        def _():
            conv[WIN, :cols] = jnp.zeros((cols, chans), F32)

        @pl.when(tile == n_tiles - 1)
        def _():
            conv[WIN + rows + 1, :cols] = jnp.zeros((cols, chans), F32)

    def cut_all(frame):
        def cut(slot, carry):
            within = reversed_bits(slot, levels)
            for group_at in range(n_frames):
                for extra in range(blk_dev):
                    block = group_at * per_group + within * blk_dev + extra
                    local = (owners[block] - tile) * rows + row_off[frame, block] - REACH
                    first = jnp.clip(local + 1, -WIN, rows + 2) + WIN
                    col = col_off[frame, block]
                    lot = group_at * blk_dev + extra
                    for i in range(WIN):
                        win[lot, i * WIN : (i + 1) * WIN, :] = conv[first + i, pl.ds(col, WIN), :]
            parts[frame, slot] = win[...].astype(BF16)
            return carry

        lax.fori_loop(0, n_tiles, cut, 0)

    def combine(level, frame):
        copy, source, start, count = halving(level, frame)
        copy.wait_recv()

        def add(i, carry):
            both = source[frame, start + i].astype(F32) + lands[level][frame, i].astype(F32)
            sums[level][frame, i] = both.astype(BF16)
            return carry

        lax.fori_loop(0, count, add, 0)
        if level + 1 < levels:
            halving(level + 1, frame)[0].start()
        else:
            for step in range(n_frames - 1):
                handing(step, frame, group).start()
            out[group * frame_dev + frame] = sums[level][frame, 0, pl.ds(group * blk_dev, blk_dev)]

    convolve(0)
    cut_all(0)
    pl.semaphore_wait(barrier, len(partners) + len(peers))
    halving(0, 0)[0].start()

    def advance(turn, carry):
        @pl.when(turn < frame_dev)
        def _():
            convolve(turn)

        @pl.when(turn <= frame_dev)
        def _():
            combine(0, turn - 1)

        @pl.when(turn < frame_dev)
        def _():
            cut_all(turn)
            halving(0, turn)[0].start()

        for level in reversed(range(1, levels)):
            frame = turn - 1 - level

            @pl.when((frame >= 0) & (frame < frame_dev))
            def _():
                combine(level, frame)

        return carry

    lax.fori_loop(1, frame_dev + levels, advance, 0)
    for frame in range(frame_dev):
        for level in range(levels):
            halving(level, frame)[0].wait_send()
        for step in range(n_frames - 1):
            handing(step, frame, (group + n_frames - step - 1) % n_frames).wait()


def rms_scale(values, gain):
    return values * lax.rsqrt(jnp.mean(values * values, axis=-1, keepdims=True) + 1e-06) * gain


def token_kernel(
    bundle, patch, query, starts, w_corr, w_feat, time_embed, gain_attn, w_qkv, w_attn_out, gain_mlp,
    w_up, w_down, out, tokens, w_token, w_qkv_t,
):
    step = pl.program_id(0)
    frames, _, cells, chans = patch.shape
    width = w_feat.shape[1]
    head = width // HEADS
    span = GROUP * frames
    per_block = QBLK // (GROUP * bundle)

    @pl.when(step == 0)
    def _():
        w_token[:chans] = jnp.zeros((chans, width), BF16)
        w_token[: w_corr.shape[0]] = w_corr[...]
        w_token[chans:] = w_feat[...]
        w_qkv_t[...] = w_qkv[...].T

    @pl.when(step % per_block == 0)
    def _():
        queries = query[...]
        blank = jnp.zeros((chans - cells, chans), BF16)
        for some in range(0, frames, 4):
            corrs = []
            for frame in range(some, some + 4):
                window = jnp.concatenate([patch[frame, 0], blank], axis=0)
                corr = lax.dot_general(
                    queries, window, (((1,), (1,)), ((), ())), preferred_element_type=F32
                ) * chans ** (-0.5)
                corrs.append(jnp.concatenate([corr.astype(BF16), queries], axis=1))
            made = jnp.dot(jnp.concatenate(corrs, axis=0), w_token[...], preferred_element_type=F32)
            for n in range(4):
                tokens[some + n] = made[n * QBLK : (n + 1) * QBLK] + time_embed[some + n : some + n + 1, :]

    first = (step % per_block) * (GROUP * bundle)
    x = jnp.concatenate(
        [
            tokens[:, pl.ds(pl.multiple_of(first + GROUP * g, GROUP), GROUP), :].reshape(span, width)
            for g in range(bundle)
        ],
        axis=0,
    )
    normed = rms_scale(x, gain_attn[...]).astype(BF16)
    qkv = lax.dot_general(
        w_qkv_t[...], normed, (((1,), (1,)), ((), ())), preferred_element_type=F32
    ).astype(BF16)
    key_at = lax.broadcasted_iota(jnp.int32, (span, span), 0)
    query_at = lax.broadcasted_iota(jnp.int32, (span, span), 1)
    same = (key_at % GROUP) == (query_at % GROUP)
    power = head ** (-0.5) * math.log2(math.e)
    start_rows = jnp.broadcast_to(starts[...].astype(F32)[None, :], (GROUP, QBLK)).astype(BF16)
    source = lax.broadcasted_iota(jnp.int32, (QBLK, span), 0)
    track = lax.broadcasted_iota(jnp.int32, (QBLK, span), 1) % GROUP
    gathered = []
    for g in range(bundle):
        at = slice(g * span, (g + 1) * span)
        pick = (source == track + (first + GROUP * g)).astype(BF16)
        start = jnp.dot(start_rows, pick, preferred_element_type=F32)[:1].astype(jnp.int32)
        valid = same & ((key_at // GROUP) >= start)
        scores = [
            lax.dot_general(
                qkv[width + h * head : width + (h + 1) * head, at],
                qkv[h * head : (h + 1) * head, at],
                (((0,), (0,)), ((), ())),
                preferred_element_type=F32,
            )
            for h in range(HEADS)
        ]
        weights, totals = [], []
        for h in range(HEADS):
            score = jnp.where(valid, scores[h], -1e30)
            weight = jnp.exp2((score - jnp.max(score, axis=0, keepdims=True)) * power)
            totals.append(jnp.sum(weight, axis=0, keepdims=True))
            weights.append(weight.astype(BF16))
        heads = [
            jnp.dot(
                qkv[2 * width + h * head : 2 * width + (h + 1) * head, at],
                weights[h],
                preferred_element_type=F32,
            )
            for h in range(HEADS)
        ]
        gathered.append(
            jnp.concatenate([(heads[h] / totals[h]).astype(BF16) for h in range(HEADS)], axis=0)
        )
    attended = jnp.concatenate(gathered, axis=1)
    mixed = x + lax.dot_general(
        attended, w_attn_out[...], (((0,), (0,)), ((), ())), preferred_element_type=F32
    )
    normed2 = rms_scale(mixed, gain_mlp[...]).astype(BF16)
    hidden = jax.nn.gelu(
        jnp.dot(normed2, w_up[...], preferred_element_type=F32), approximate=True
    ).astype(BF16)
    result = mixed + jnp.dot(hidden, w_down[...], preferred_element_type=F32)
    result = result.astype(BF16)
    move = (query_at == (key_at % frames) * GROUP + key_at // frames).astype(BF16)
    for g in range(bundle):
        at = slice(g * span, (g + 1) * span)
        out[at, :] = jnp.dot(move, result[at, :], preferred_element_type=F32).astype(BF16)


def body(
    features, w_conv, query_feats, offset_rows, offset_cols, owners, start_frames, w_corr, w_feat,
    time_embed, gain_attn, w_qkv, w_attn_out, gain_mlp, w_up, w_down,
):
    n_tiles = lax.axis_size("tiles")
    n_frames = lax.axis_size("frames")
    frame_dev, rows, cols, chans = features.shape
    blocks = owners.shape[0]
    blk_dev = blocks // (n_frames * n_tiles)
    lots = n_frames * blk_dev
    levels = n_tiles.bit_length() - 1
    frames_total = frame_dev * n_frames
    width = w_feat.shape[1]
    whole = pl.BlockSpec(memory_space=pltpu.VMEM)
    scalars = pl.BlockSpec(memory_space=pltpu.SMEM)

    halves = [
        pltpu.VMEM((frame_dev, n_tiles >> (level + 1), lots, CELLS, chans), BF16)
        for level in range(levels)
    ]
    patch = pl.pallas_call(
        functools.partial(window_kernel, n_tiles, n_frames),
        out_shape=jax.ShapeDtypeStruct((frames_total, blk_dev, CELLS, chans), BF16),
        in_specs=[scalars, scalars, scalars, pl.BlockSpec(memory_space=pl.ANY), whole],
        out_specs=whole,
        scratch_shapes=[
            pltpu.VMEM((3 * chans, 3 * chans), BF16),
            pltpu.VMEM((frame_dev, rows + 4, cols, chans), BF16),
            pltpu.VMEM((rows + 2 + 2 * WIN, cols + 16, chans), F32),
            pltpu.VMEM((lots, CELLS, chans), F32),
            pltpu.VMEM((frame_dev, n_tiles, lots, CELLS, chans), BF16),
        ]
        + halves
        + halves
        + [pltpu.SemaphoreType.DMA((frame_dev,))]
        + [pltpu.SemaphoreType.DMA((levels, frame_dev))] * 2
        + [pltpu.SemaphoreType.DMA((n_frames - 1, frame_dev))] * 2,
        compiler_params=pltpu.CompilerParams(collective_id=0, has_side_effects=True),
    )(owners[:, 0], offset_rows, offset_cols, features, w_conv)

    bundle = 4
    span = GROUP * frames_total
    tracks = blk_dev * QBLK
    per_block = QBLK // (GROUP * bundle)
    def fixed(shape):
        return pl.BlockSpec(shape, lambda s: (0,) * len(shape))

    refined = pl.pallas_call(
        functools.partial(token_kernel, bundle),
        grid=(tracks // (GROUP * bundle),),
        out_shape=jax.ShapeDtypeStruct((tracks * frames_total, width), BF16),
        in_specs=[
            pl.BlockSpec((frames_total, 1, CELLS, chans), lambda s: (0, s // per_block, 0, 0)),
            pl.BlockSpec((QBLK, chans), lambda s: (s // per_block, 0)),
            pl.BlockSpec((QBLK,), lambda s: (s // per_block,)),
            fixed(w_corr.shape),
            fixed(w_feat.shape),
            fixed(time_embed.shape),
            fixed((width,)),
            fixed(w_qkv.shape),
            fixed(w_attn_out.shape),
            fixed((width,)),
            fixed(w_up.shape),
            fixed(w_down.shape),
        ],
        out_specs=pl.BlockSpec((bundle * span, width), lambda s: (s, 0)),
        scratch_shapes=[
            pltpu.VMEM((frames_total, QBLK, width), F32),
            pltpu.VMEM((2 * chans, width), BF16),
            pltpu.VMEM((3 * width, width), BF16),
        ],
    )(
        patch, query_feats, start_frames, w_corr, w_feat, time_embed, gain_attn, w_qkv,
        w_attn_out, gain_mlp, w_up, w_down,
    )
    return refined.reshape(tracks, frames_total, width)


def solution(mesh):
    placed = (
        P("frames", "tiles", None, None),
        P(),
        P(("frames", "tiles"), None),
        P("frames", None),
        P("frames", None),
        P(),
        P(("frames", "tiles")),
    ) + (P(),) * 9
    return jax.shard_map(
        body,
        mesh=mesh,
        in_specs=placed,
        out_specs=P(("frames", "tiles"), None, None),
        check_vma=False,
    )
```

profile of v0, /device:TPU:0, one launch (start us, length us, event | category | flops | bytes accessed | tf_op | source)
XLA Modules:
  0.0 67.1 jit_solution(811470303994260259)
XLA Ops:
  0.0 44.3 %shard_map.154.patch = bf16[16,1,88,128]{3,2,1,0:T(8,128)(2,1)} custom-call(s32[32]{0:T(128)} %bitcast.2, s32[4,32]{1,0:T(4,128)} %row_off.1, s32[4,32]{1,0:T(4,128)} %col_off.1, bf16[4,8,480,128]{3,2,1,0:T(8,128)(2,1)} %feat.1, bf16[3,3,128,128]{3,2,1,0:T(8,128)(2,1)} %w_conv.1), custom_call_target="tpu_custom_call" | custom-call | tf_op jit(solution)/shard_map/pallas_call | solution.py:311
  44.3 22.8 %shard_map.155 = bf16[2048,384]{1,0:T(8,128)(2,1)} custom-call(bf16[16,1,88,128]{3,2,1,0:T(8,128)(2,1)} %shard_map.154.patch, bf16[128,128]{1,0:T(8,128)(2,1)} %query.1, s32[128]{0:T(128)} %starts.1, bf16[81,384]{1,0:T(8,128)(2,1)} %w_corr.1, bf16[128,384]{1,0:T(8,128)(2,1)} %w_feat.1, f32[16,384]{1,0:T(8,128)} %time_embed.1, f32[384]{0:T(512)} %gain_attn.1, ...), custom_call_target="tpu_custom_call" | custom-call | tf_op jit(solution)/shard_map/pallas_call | solution.py:338
where the time goes:
time: 67.3 us; the launch traced here: 67.1 us
  Pallas kernels  67.1 us (100%)
    pallas_call x1, Pallas kernels, body(): pl.pallas_call(functools.partial(window_kernel, n_tiles, n_frames), out_s...  44.3 us
    pallas_call x1, Pallas kernels, body(): pl.pallas_call(functools.partial(token_kernel, bundle), grid=(tracks // (...  22.8 us

commit v1 on v0

--- a/solution.py
+++ b/solution.py
@@ -19,37 +19,34 @@
 MESH = pl.DeviceIdType.MESH
 
 
-def reversed_bits(value, bits):
-    out = value * 0
-    for bit in range(bits):
-        out = out + ((value // 2**bit) % 2) * 2 ** (bits - 1 - bit)
-    return out
-
-
 def window_kernel(
-    n_tiles, n_frames, owners, row_off, col_off, feat, w_conv, out, w_cat, padded, conv, win, parts, *scratch
+    n_tiles, n_frames, owners, row_off, col_off, feat, w_conv, out, w_cat, padded, conv, win, parts, pairs, sums,
+    lands, total, ready, feat_sem, pair_send, pair_recv, hop_send, hop_recv, out_send, out_recv,
 ):
-    levels = n_tiles.bit_length() - 1
-    sums, lands = scratch[:levels], scratch[levels : 2 * levels]
-    feat_sem, send_sem, recv_sem, out_send, out_recv = scratch[2 * levels :]
     tile, group = lax.axis_index("tiles"), lax.axis_index("frames")
     frame_dev, rows, cols, chans = feat.shape
     blocks = owners.shape[0]
     per_group = blocks // n_frames
     blk_dev = out.shape[1]
+    lots = n_frames * blk_dev
+    area = WIN * WIN
+    chips = n_tiles // 2
+    chip, core = tile // 2, tile % 2
+    first_half = 1 - (2 * chip) // chips
+    near = (1 - first_half) * (chips - 1 - chip) + first_half * chip
+    far = chips - 1 - near
+    near_way, far_way = 1 - first_half, first_half
 
     def fetch(frame):
         return pltpu.make_async_copy(feat.at[frame], padded.at[frame, pl.ds(2, rows)], feat_sem.at[frame])
 
     for frame in range(frame_dev):
         fetch(frame).start()
-    partners = []
-    for level in range(levels):
-        bit = (tile // 2**level) % 2
-        partners.append((group, tile + (1 - 2 * bit) * 2**level))
+    partner = (group, tile + 1 - 2 * core)
+    sides = [(group, (tile + 2) % n_tiles), (group, (tile + n_tiles - 2) % n_tiles)]
     peers = [((group + step) % n_frames, tile) for step in range(1, n_frames)]
     barrier = pltpu.get_barrier_semaphore()
-    for device in partners + peers:
+    for device in [partner] + sides + peers:
         pl.semaphore_signal(barrier, inc=1, device_id=device, device_id_type=MESH)
 
     blank = jnp.zeros((2, cols, chans), BF16)
@@ -57,6 +54,7 @@
         padded[frame, 0:2] = blank
         padded[frame, rows + 2 : rows + 4] = blank
     win[...] = jnp.zeros_like(win)
+    total[...] = jnp.zeros_like(total)
     for y in range(WIN):
         conv[y] = jnp.zeros(conv.shape[1:], F32)
         conv[WIN + rows + 2 + y] = jnp.zeros(conv.shape[1:], F32)
@@ -65,23 +63,29 @@
         for b in range(3):
             w_cat[a * chans : (a + 1) * chans, b * chans : (b + 1) * chans] = w_conv[a, b]
 
-    def halving(level, frame):
-        source = parts if level == 0 else sums[level - 1]
-        count = n_tiles >> (level + 1)
-        bit = (tile // 2**level) % 2
-        copy = pltpu.make_async_remote_copy(
-            src_ref=source.at[frame, pl.ds((1 - bit) * count, count)],
-            dst_ref=lands[level].at[frame],
-            send_sem=send_sem.at[level, frame],
-            recv_sem=recv_sem.at[level, frame],
-            device_id=partners[level],
+    def pairing(frame, dest):
+        return pltpu.make_async_remote_copy(
+            src_ref=parts.at[frame, 2 * dest + 1 - core],
+            dst_ref=pairs.at[frame, dest],
+            send_sem=pair_send.at[frame, dest],
+            recv_sem=pair_recv.at[frame, dest],
+            device_id=partner,
             device_id_type=MESH,
         )
-        return copy, source, bit * count, count
+
+    def hop(way, frame, dest):
+        return pltpu.make_async_remote_copy(
+            src_ref=sums.at[frame, dest],
+            dst_ref=lands.at[way, frame, dest],
+            send_sem=hop_send.at[frame, dest],
+            recv_sem=hop_recv.at[way, frame, dest],
+            device_id=(group, (tile + n_tiles + 2 - 4 * way) % n_tiles),
+            device_id_type=MESH,
+        )
 
     def handing(step, frame, giver):
         return pltpu.make_async_remote_copy(
-            src_ref=sums[levels - 1].at[frame, 0, pl.ds(peers[step][0] * blk_dev, blk_dev)],
+            src_ref=ready.at[frame, pl.ds(peers[step][0] * blk_dev, blk_dev)],
             dst_ref=out.at[giver * frame_dev + frame],
             send_sem=out_send.at[step, frame],
             recv_sem=out_recv.at[step, frame],
@@ -114,71 +118,114 @@
             conv[WIN + rows + 1, :cols] = jnp.zeros((cols, chans), F32)
 
     def cut_all(frame):
-        def cut(slot, carry):
-            within = reversed_bits(slot, levels)
-            for group_at in range(n_frames):
-                for extra in range(blk_dev):
-                    block = group_at * per_group + within * blk_dev + extra
-                    local = (owners[block] - tile) * rows + row_off[frame, block] - REACH
-                    first = jnp.clip(local + 1, -WIN, rows + 2) + WIN
-                    col = col_off[frame, block]
-                    lot = group_at * blk_dev + extra
-                    for i in range(WIN):
-                        win[lot, i * WIN : (i + 1) * WIN, :] = conv[first + i, pl.ds(col, WIN), :]
-            parts[frame, slot] = win[...].astype(BF16)
+        def cut(turn, carry):
+            dest = (1 - first_half) * turn + first_half * (chips - 1 - turn)
+            for side in range(2):
+                slot = 2 * dest + side
+                for group_at in range(n_frames):
+                    for extra in range(blk_dev):
+                        block = group_at * per_group + slot * blk_dev + extra
+                        local = (owners[block] - tile) * rows + row_off[frame, block] - REACH
+                        first = jnp.clip(local + 1, -WIN, rows + 2) + WIN
+                        col = col_off[frame, block]
+                        at = (group_at * blk_dev + extra) * area
+                        for i in range(WIN):
+                            win[side, at + i * WIN : at + (i + 1) * WIN, :] = conv[first + i, pl.ds(col, WIN), :]
+                parts[frame, slot] = win[side].astype(BF16)
+            pairing(frame, dest).start()
             return carry
 
-        lax.fori_loop(0, n_tiles, cut, 0)
-
-    def combine(level, frame):
-        copy, source, start, count = halving(level, frame)
-        copy.wait_recv()
-
-        def add(i, carry):
-            both = source[frame, start + i].astype(F32) + lands[level][frame, i].astype(F32)
-            sums[level][frame, i] = both.astype(BF16)
+        lax.fori_loop(0, chips, cut, 0)
+
+    def own(frame, dest):
+        pairing(frame, dest).wait_recv()
+        return parts[frame, 2 * dest + core].astype(F32) + pairs[frame, dest].astype(F32)
+
+    def move(way, frame):
+        upstream = (1 - way) * chip + way * (chips - 1 - chip)
+
+        def one(i, carry):
+            dest = (1 - way) * (chips - 1 - i) + way * i
+            mine = own(frame, dest)
+
+            @pl.when(upstream > 0)
+            def _():
+                hop(way, frame, dest).wait_recv()
+                sums[frame, dest] = (mine + lands[way, frame, dest].astype(F32)).astype(BF16)
+
+            @pl.when(upstream == 0)
+            def _():
+                sums[frame, dest] = mine.astype(BF16)
+
+            hop(way, frame, dest).start()
             return carry
 
-        lax.fori_loop(0, count, add, 0)
-        if level + 1 < levels:
-            halving(level + 1, frame)[0].start()
-        else:
-            for step in range(n_frames - 1):
-                handing(step, frame, group).start()
-            out[group * frame_dev + frame] = sums[level][frame, 0, pl.ds(group * blk_dev, blk_dev)]
+        lax.fori_loop(0, chips - 1 - upstream, one, 0)
+
+    def finish(frame):
+        span = parts.shape[2]
+        total[:span] = own(frame, chip)
+
+        @pl.when(chip > 0)
+        def _():
+            hop(0, frame, chip).wait_recv()
+            total[:span] = total[:span] + lands[0, frame, chip].astype(F32)
+
+        @pl.when(chip < chips - 1)
+        def _():
+            hop(1, frame, chip).wait_recv()
+            total[:span] = total[:span] + lands[1, frame, chip].astype(F32)
+
+        for lot in range(lots):
+            ready[frame, lot] = total[lot * area : lot * area + CELLS].astype(BF16)
+        for step in range(n_frames - 1):
+            handing(step, frame, group).start()
+        out[group * frame_dev + frame] = ready[frame, pl.ds(group * blk_dev, blk_dev)]
 
     convolve(0)
-    cut_all(0)
-    pl.semaphore_wait(barrier, len(partners) + len(peers))
-    halving(0, 0)[0].start()
+    pl.semaphore_wait(barrier, 1 + len(sides) + len(peers))
 
     def advance(turn, carry):
+        @pl.when((turn > 0) & (turn < frame_dev))
+        def _():
+            convolve(turn)
+
         @pl.when(turn < frame_dev)
         def _():
-            convolve(turn)
-
-        @pl.when(turn <= frame_dev)
-        def _():
-            combine(0, turn - 1)
-
-        @pl.when(turn < frame_dev)
-        def _():
             cut_all(turn)
-            halving(0, turn)[0].start()
-
-        for level in reversed(range(1, levels)):
-            frame = turn - 1 - level
-
-            @pl.when((frame >= 0) & (frame < frame_dev))
+
+            @pl.when(near == 0)
             def _():
-                combine(level, frame)
+                move(near_way, turn)
+
+        late = turn - far
+
+        @pl.when((late >= 0) & (late < frame_dev))
+        def _():
+            finish(late)
+            move(far_way, late)
+
+        soon = turn - near
+
+        @pl.when((near > 0) & (soon >= 0) & (soon < frame_dev))
+        def _():
+            move(near_way, soon)
 
         return carry
 
-    lax.fori_loop(1, frame_dev + levels, advance, 0)
+    lax.fori_loop(0, frame_dev + chips - 1, advance, 0)
     for frame in range(frame_dev):
-        for level in range(levels):
-            halving(level, frame)[0].wait_send()
+
+        def drain(dest, carry):
+            pairing(frame, dest).wait_send()
+
+            @pl.when(dest != chip)
+            def _():
+                hop(0, frame, dest).wait_send()
+
+            return carry
+
+        lax.fori_loop(0, chips, drain, 0)
         for step in range(n_frames - 1):
             handing(step, frame, (group + n_frames - step - 1) % n_frames).wait()
 
@@ -298,16 +345,14 @@
     blocks = owners.shape[0]
     blk_dev = blocks // (n_frames * n_tiles)
     lots = n_frames * blk_dev
-    levels = n_tiles.bit_length() - 1
     frames_total = frame_dev * n_frames
     width = w_feat.shape[1]
     whole = pl.BlockSpec(memory_space=pltpu.VMEM)
     scalars = pl.BlockSpec(memory_space=pltpu.SMEM)
 
-    halves = [
-        pltpu.VMEM((frame_dev, n_tiles >> (level + 1), lots, CELLS, chans), BF16)
-        for level in range(levels)
-    ]
+    chips = n_tiles // 2
+    span_rows = -(-lots * WIN * WIN // 8) * 8
+    total_rows = -(-((lots - 1) * WIN * WIN + CELLS) // 8) * 8
     patch = pl.pallas_call(
         functools.partial(window_kernel, n_tiles, n_frames),
         out_shape=jax.ShapeDtypeStruct((frames_total, blk_dev, CELLS, chans), BF16),
@@ -317,13 +362,17 @@
             pltpu.VMEM((3 * chans, 3 * chans), BF16),
             pltpu.VMEM((frame_dev, rows + 4, cols, chans), BF16),
             pltpu.VMEM((rows + 2 + 2 * WIN, cols + 16, chans), F32),
-            pltpu.VMEM((lots, CELLS, chans), F32),
-            pltpu.VMEM((frame_dev, n_tiles, lots, CELLS, chans), BF16),
+            pltpu.VMEM((2, span_rows, chans), F32),
+            pltpu.VMEM((frame_dev, n_tiles, span_rows, chans), BF16),
+            pltpu.VMEM((frame_dev, chips, span_rows, chans), BF16),
+            pltpu.VMEM((frame_dev, chips, span_rows, chans), BF16),
+            pltpu.VMEM((2, frame_dev, chips, span_rows, chans), BF16),
+            pltpu.VMEM((total_rows, chans), F32),
+            pltpu.VMEM((frame_dev, lots, CELLS, chans), BF16),
         ]
-        + halves
-        + halves
         + [pltpu.SemaphoreType.DMA((frame_dev,))]
-        + [pltpu.SemaphoreType.DMA((levels, frame_dev))] * 2
+        + [pltpu.SemaphoreType.DMA((frame_dev, chips))] * 3
+        + [pltpu.SemaphoreType.DMA((2, frame_dev, chips))]
         + [pltpu.SemaphoreType.DMA((n_frames - 1, frame_dev))] * 2,
         compiler_params=pltpu.CompilerParams(collective_id=0, has_side_effects=True),
     )(owners[:, 0], offset_rows, offset_cols, features, w_conv)

time: 67.3 us -> 67.7 us (level)
  no operation moved by 1% of the time
where the time goes in v1:
time: 67.7 us; the launch traced here: 67.6 us
  Pallas kernels  67.6 us (100%)
    pallas_call x1, Pallas kernels, body(): pl.pallas_call(functools.partial(window_kernel, n_tiles, n_frames), out_s...  44.8 us
    pallas_call x1, Pallas kernels, body(): pl.pallas_call(functools.partial(token_kernel, bundle), grid=(tracks // (...  22.8 us

profile of v1, /device:TPU:0, one launch (start us, length us, event | category | flops | bytes accessed | tf_op | source)
XLA Modules:
  0.0 67.6 jit_solution(15852860215144105652)
XLA Ops:
  0.0 44.8 %shard_map.154.patch = bf16[16,1,88,128]{3,2,1,0:T(8,128)(2,1)} custom-call(s32[32]{0:T(128)} %bitcast.2, s32[4,32]{1,0:T(4,128)} %row_off.1, s32[4,32]{1,0:T(4,128)} %col_off.1, bf16[4,8,480,128]{3,2,1,0:T(8,128)(2,1)} %feat.1, bf16[3,3,128,128]{3,2,1,0:T(8,128)(2,1)} %w_conv.1), custom_call_target="tpu_custom_call" | custom-call | tf_op jit(solution)/shard_map/pallas_call | solution.py:356
  44.8 22.8 %shard_map.155 = bf16[2048,384]{1,0:T(8,128)(2,1)} custom-call(bf16[16,1,88,128]{3,2,1,0:T(8,128)(2,1)} %shard_map.154.patch, bf16[128,128]{1,0:T(8,128)(2,1)} %query.1, s32[128]{0:T(128)} %starts.1, bf16[81,384]{1,0:T(8,128)(2,1)} %w_corr.1, bf16[128,384]{1,0:T(8,128)(2,1)} %w_feat.1, f32[16,384]{1,0:T(8,128)} %time_embed.1, f32[384]{0:T(512)} %gain_attn.1, ...), custom_call_target="tpu_custom_call" | custom-call | tf_op jit(solution)/shard_map/pallas_call | solution.py:387

commit v2 on v1

--- a/solution.py
+++ b/solution.py
@@ -20,8 +20,8 @@
 
 
 def window_kernel(
-    n_tiles, n_frames, owners, row_off, col_off, feat, w_conv, out, w_cat, padded, conv, win, parts, pairs, sums,
-    lands, total, ready, feat_sem, pair_send, pair_recv, hop_send, hop_recv, out_send, out_recv,
+    n_tiles, n_frames, owners_in, row_in, col_in, feat, w_conv_in, out, owners, row_off, col_off, w_conv, w_cat, padded,
+    conv, win, parts, pairs, sums, lands, total, ready, load_sem, feat_sem, pair_send, pair_recv, hop_send, hop_recv, out_send, out_recv,
 ):
     tile, group = lax.axis_index("tiles"), lax.axis_index("frames")
     frame_dev, rows, cols, chans = feat.shape
@@ -40,7 +40,16 @@
     def fetch(frame):
         return pltpu.make_async_copy(feat.at[frame], padded.at[frame, pl.ds(2, rows)], feat_sem.at[frame])
 
-    for frame in range(frame_dev):
+    loads = [
+        pltpu.make_async_copy(source, target, load_sem.at[n])
+        for n, (source, target) in enumerate(
+            [(w_conv_in, w_conv), (owners_in, owners), (row_in, row_off), (col_in, col_off)]
+        )
+    ]
+    fetch(0).start()
+    for load in loads:
+        load.start()
+    for frame in range(1, frame_dev):
         fetch(frame).start()
     partner = (group, tile + 1 - 2 * core)
     sides = [(group, (tile + 2) % n_tiles), (group, (tile + n_tiles - 2) % n_tiles)]
@@ -59,6 +68,8 @@
         conv[y] = jnp.zeros(conv.shape[1:], F32)
         conv[WIN + rows + 2 + y] = jnp.zeros(conv.shape[1:], F32)
     conv[WIN : WIN + rows + 2, cols:] = jnp.zeros((rows + 2, conv.shape[1] - cols, chans), F32)
+    for load in loads:
+        load.wait()
     for a in range(3):
         for b in range(3):
             w_cat[a * chans : (a + 1) * chans, b * chans : (b + 1) * chans] = w_conv[a, b]
@@ -235,8 +246,8 @@
 
 
 def token_kernel(
-    bundle, patch, query, starts, w_corr, w_feat, time_embed, gain_attn, w_qkv, w_attn_out, gain_mlp,
-    w_up, w_down, out, tokens, w_token, w_qkv_t,
+    bundle, steps, patch, query, starts, w_corr, w_feat, time_embed, gain_attn, w_qkv, w_attn_out, gain_mlp,
+    w_up, w_down, out, tokens, w_token, w_qkv_t, mixed, hidden,
 ):
     step = pl.program_id(0)
     frames, _, cells, chans = patch.shape
@@ -244,6 +255,9 @@
     head = width // HEADS
     span = GROUP * frames
     per_block = QBLK // (GROUP * bundle)
+    units = w_up.shape[1]
+    lump = 4 * chans
+    down = 2
 
     @pl.when(step == 0)
     def _():
@@ -252,7 +266,7 @@
         w_token[chans:] = w_feat[...]
         w_qkv_t[...] = w_qkv[...].T
 
-    @pl.when(step % per_block == 0)
+    @pl.when((step % per_block == 0) & (step < steps))
     def _():
         queries = query[...]
         blank = jnp.zeros((chans - cells, chans), BF16)
@@ -266,73 +280,135 @@
                 corrs.append(jnp.concatenate([corr.astype(BF16), queries], axis=1))
             made = jnp.dot(jnp.concatenate(corrs, axis=0), w_token[...], preferred_element_type=F32)
             for n in range(4):
-                tokens[some + n] = made[n * QBLK : (n + 1) * QBLK] + time_embed[some + n : some + n + 1, :]
-
-    first = (step % per_block) * (GROUP * bundle)
-    x = jnp.concatenate(
-        [
-            tokens[:, pl.ds(pl.multiple_of(first + GROUP * g, GROUP), GROUP), :].reshape(span, width)
-            for g in range(bundle)
-        ],
-        axis=0,
-    )
-    normed = rms_scale(x, gain_attn[...]).astype(BF16)
-    qkv = lax.dot_general(
-        w_qkv_t[...], normed, (((1,), (1,)), ((), ())), preferred_element_type=F32
-    ).astype(BF16)
+                whole = made[n * QBLK : (n + 1) * QBLK] + time_embed[some + n : some + n + 1, :]
+                for plane in range(width // chans):
+                    tokens[plane, pl.ds(some + n, QBLK, stride=frames), :] = whole[
+                        :, plane * chans : (plane + 1) * chans
+                    ]
+
     key_at = lax.broadcasted_iota(jnp.int32, (span, span), 0)
     query_at = lax.broadcasted_iota(jnp.int32, (span, span), 1)
-    same = (key_at % GROUP) == (query_at % GROUP)
-    power = head ** (-0.5) * math.log2(math.e)
-    start_rows = jnp.broadcast_to(starts[...].astype(F32)[None, :], (GROUP, QBLK)).astype(BF16)
-    source = lax.broadcasted_iota(jnp.int32, (QBLK, span), 0)
-    track = lax.broadcasted_iota(jnp.int32, (QBLK, span), 1) % GROUP
-    gathered = []
-    for g in range(bundle):
-        at = slice(g * span, (g + 1) * span)
-        pick = (source == track + (first + GROUP * g)).astype(BF16)
-        start = jnp.dot(start_rows, pick, preferred_element_type=F32)[:1].astype(jnp.int32)
-        valid = same & ((key_at // GROUP) >= start)
-        scores = [
-            lax.dot_general(
-                qkv[width + h * head : width + (h + 1) * head, at],
-                qkv[h * head : (h + 1) * head, at],
+
+    def attention():
+        first = (step % per_block) * (GROUP * bundle)
+        lines = pl.ds(pl.multiple_of(first * frames, span), bundle * span)
+        x = jnp.concatenate([tokens[plane, lines, :] for plane in range(width // chans)], axis=1)
+        normed = rms_scale(x, gain_attn[...]).astype(BF16)
+        qkv = lax.dot_general(
+            w_qkv_t[...], normed, (((1,), (1,)), ((), ())), preferred_element_type=F32
+        ).astype(BF16)
+        same = (key_at // frames) == (query_at // frames)
+        power = head ** (-0.5) * math.log2(math.e)
+        start_rows = jnp.broadcast_to(starts[...].astype(F32)[None, :], (GROUP, QBLK)).astype(BF16)
+        source = lax.broadcasted_iota(jnp.int32, (QBLK, span), 0)
+        track = lax.broadcasted_iota(jnp.int32, (QBLK, span), 1) // frames
+        nothing = jnp.zeros((head, span), BF16)
+        yield
+        heads, scored, weighed = {}, {}, {}
+
+        def score_pair(g, h):
+            at = slice(g * span, (g + 1) * span)
+            one = qkv[h * head : (h + 1) * head, at]
+            two = qkv[(h + 1) * head : (h + 2) * head, at]
+            pair = jnp.concatenate(
+                [jnp.concatenate([one, nothing], axis=1), jnp.concatenate([nothing, two], axis=1)], axis=0
+            )
+            scored[g, h] = lax.dot_general(
+                qkv[width + h * head : width + (h + 2) * head, at],
+                pair,
                 (((0,), (0,)), ((), ())),
                 preferred_element_type=F32,
             )
-            for h in range(HEADS)
-        ]
-        weights, totals = [], []
-        for h in range(HEADS):
-            score = jnp.where(valid, scores[h], -1e30)
+
+        def weigh_pair(g, h):
+            if h == 0:
+                pick = (source == track + (first + GROUP * g)).astype(BF16)
+                start = jnp.dot(start_rows, pick, preferred_element_type=F32)[:1].astype(jnp.int32)
+                valid = same & ((key_at % frames) >= start)
+                masks[g] = jnp.concatenate([valid, valid], axis=1)
+            score = jnp.where(masks[g], scored.pop((g, h)), -1e30)
             weight = jnp.exp2((score - jnp.max(score, axis=0, keepdims=True)) * power)
-            totals.append(jnp.sum(weight, axis=0, keepdims=True))
-            weights.append(weight.astype(BF16))
-        heads = [
-            jnp.dot(
-                qkv[2 * width + h * head : 2 * width + (h + 1) * head, at],
-                weights[h],
-                preferred_element_type=F32,
+            weighed[g, h] = weight.astype(BF16), jnp.sum(weight, axis=0, keepdims=True)
+
+        def value_pair(g, h):
+            at = slice(g * span, (g + 1) * span)
+            weight, sums = weighed.pop((g, h))
+            both = jnp.dot(
+                qkv[2 * width + h * head : 2 * width + (h + 2) * head, at], weight, preferred_element_type=F32
             )
-            for h in range(HEADS)
-        ]
-        gathered.append(
-            jnp.concatenate([(heads[h] / totals[h]).astype(BF16) for h in range(HEADS)], axis=0)
+            heads[g, h] = (both[:head, :span] / sums[:, :span]).astype(BF16)
+            heads[g, h + 1] = (both[head:, span:] / sums[:, span:]).astype(BF16)
+
+        masks = {}
+        pairs = [(g, h) for g in range(bundle) for h in range(0, HEADS, 2)]
+        lead = 2
+        for n in range(len(pairs) + 2 * lead):
+            if n < len(pairs):
+                score_pair(*pairs[n])
+            if 0 <= n - lead < len(pairs):
+                weigh_pair(*pairs[n - lead])
+            if 0 <= n - 2 * lead < len(pairs):
+                value_pair(*pairs[n - 2 * lead])
+            if n < len(pairs):
+                yield
+        gathered = [jnp.concatenate([heads[g, h] for h in range(HEADS)], axis=0) for g in range(bundle)]
+        attended = jnp.concatenate(gathered, axis=1)
+        mixed[step % 2] = x + lax.dot_general(
+            attended, w_attn_out[...], (((0,), (0,)), ((), ())), preferred_element_type=F32
         )
-    attended = jnp.concatenate(gathered, axis=1)
-    mixed = x + lax.dot_general(
-        attended, w_attn_out[...], (((0,), (0,)), ((), ())), preferred_element_type=F32
-    )
-    normed2 = rms_scale(mixed, gain_mlp[...]).astype(BF16)
-    hidden = jax.nn.gelu(
-        jnp.dot(normed2, w_up[...], preferred_element_type=F32), approximate=True
-    ).astype(BF16)
-    result = mixed + jnp.dot(hidden, w_down[...], preferred_element_type=F32)
-    result = result.astype(BF16)
-    move = (query_at == (key_at % frames) * GROUP + key_at // frames).astype(BF16)
-    for g in range(bundle):
-        at = slice(g * span, (g + 1) * span)
-        out[at, :] = jnp.dot(move, result[at, :], preferred_element_type=F32).astype(BF16)
+        yield
+
+    def feed_forward():
+        base = mixed[(step + 1) % 2]
+        normed2 = rms_scale(base, gain_mlp[...]).astype(BF16)
+        yield
+        for at in range(0, units, lump):
+            hidden[:, at : at + lump] = jax.nn.gelu(
+                jnp.dot(normed2, w_up[:, at : at + lump], preferred_element_type=F32), approximate=True
+            ).astype(BF16)
+            yield
+        for part in range(down):
+            stretch = bundle * span // down
+            lines = slice(part * stretch, (part + 1) * stretch)
+            out[lines, :] = (
+                base[lines] + jnp.dot(hidden[lines, :], w_down[...], preferred_element_type=F32)
+            ).astype(BF16)
+            yield
+
+    @pl.when(step == 0)
+    def _():
+        for _ in attention():
+            pass
+
+    @pl.when((step > 0) & (step < steps))
+    def _():
+        ahead, behind = attention(), feed_forward()
+        next(behind)
+        next(ahead)
+        total = bundle * HEADS // 2
+        parts = units // lump + down
+        done = 0
+        for n in range(total):
+            next(ahead)
+            while done < parts and (done + 1) * total <= (n + 1) * parts:
+                next(behind)
+                done += 1
+        for rest in (ahead, behind):
+            for _ in rest:
+                pass
+
+    @pl.when(step == steps)
+    def _():
+        for _ in feed_forward():
+            pass
+
+
+def grant(scratch):
+    held = 0
+    for ref in scratch:
+        if getattr(ref, "memory_space", None) == pltpu.VMEM:
+            held += math.prod(ref.shape) * jnp.dtype(ref.dtype).itemsize
+    return min(held + 6 * 2**20, 58 * 2**20)
 
 
 def body(
@@ -348,34 +424,49 @@
     frames_total = frame_dev * n_frames
     width = w_feat.shape[1]
     whole = pl.BlockSpec(memory_space=pltpu.VMEM)
-    scalars = pl.BlockSpec(memory_space=pltpu.SMEM)
 
     chips = n_tiles // 2
     span_rows = -(-lots * WIN * WIN // 8) * 8
     total_rows = -(-((lots - 1) * WIN * WIN + CELLS) // 8) * 8
+    scratch = [
+        pltpu.SMEM((blocks,), jnp.int32),
+        pltpu.SMEM((frame_dev, blocks), jnp.int32),
+        pltpu.SMEM((frame_dev, blocks), jnp.int32),
+        pltpu.VMEM(w_conv.shape, BF16),
+        pltpu.VMEM((3 * chans, 3 * chans), BF16),
+        pltpu.VMEM((frame_dev, rows + 4, cols, chans), BF16),
+        pltpu.VMEM((rows + 2 + 2 * WIN, cols + 16, chans), F32),
+        pltpu.VMEM((2, span_rows, chans), F32),
+        pltpu.VMEM((frame_dev, n_tiles, span_rows, chans), BF16),
+        pltpu.VMEM((frame_dev, chips, span_rows, chans), BF16),
+        pltpu.VMEM((frame_dev, chips, span_rows, chans), BF16),
+        pltpu.VMEM((2, frame_dev, chips, span_rows, chans), BF16),
+        pltpu.VMEM((total_rows, chans), F32),
+        pltpu.VMEM((frame_dev, lots, CELLS, chans), BF16),
+        pltpu.SemaphoreType.DMA((4,)),
+        pltpu.SemaphoreType.DMA((frame_dev,)),
+        pltpu.SemaphoreType.DMA((frame_dev, chips)),
+        pltpu.SemaphoreType.DMA((frame_dev, chips)),
+        pltpu.SemaphoreType.DMA((frame_dev, chips)),
+        pltpu.SemaphoreType.DMA((2, frame_dev, chips)),
+        pltpu.SemaphoreType.DMA((n_frames - 1, frame_dev)),
+        pltpu.SemaphoreType.DMA((n_frames - 1, frame_dev)),
+    ]
     patch = pl.pallas_call(
         functools.partial(window_kernel, n_tiles, n_frames),
         out_shape=jax.ShapeDtypeStruct((frames_total, blk_dev, CELLS, chans), BF16),
-        in_specs=[scalars, scalars, scalars, pl.BlockSpec(memory_space=pl.ANY), whole],
+        in_specs=[pl.BlockSpec(memory_space=pltpu.HBM)] * 5,
         out_specs=whole,
-        scratch_shapes=[
-            pltpu.VMEM((3 * chans, 3 * chans), BF16),
-            pltpu.VMEM((frame_dev, rows + 4, cols, chans), BF16),
-            pltpu.VMEM((rows + 2 + 2 * WIN, cols + 16, chans), F32),
-            pltpu.VMEM((2, span_rows, chans), F32),
-            pltpu.VMEM((frame_dev, n_tiles, span_rows, chans), BF16),
-            pltpu.VMEM((frame_dev, chips, span_rows, chans), BF16),
-            pltpu.VMEM((frame_dev, chips, span_rows, chans), BF16),
-            pltpu.VMEM((2, frame_dev, chips, span_rows, chans), BF16),
-            pltpu.VMEM((total_rows, chans), F32),
-            pltpu.VMEM((frame_dev, lots, CELLS, chans), BF16),
+        scratch_shapes=scratch,
+        compiler_params=pltpu.CompilerParams(
+            collective_id=0, has_side_effects=True, vmem_limit_bytes=grant(scratch)
+        ),
+    )(
+        *[
+            pltpu.with_memory_space_constraint(x, pltpu.HBM)
+            for x in (owners[:, 0], offset_rows, offset_cols, features, w_conv)
         ]
-        + [pltpu.SemaphoreType.DMA((frame_dev,))]
-        + [pltpu.SemaphoreType.DMA((frame_dev, chips))] * 3
-        + [pltpu.SemaphoreType.DMA((2, frame_dev, chips))]
-        + [pltpu.SemaphoreType.DMA((n_frames - 1, frame_dev))] * 2,
-        compiler_params=pltpu.CompilerParams(collective_id=0, has_side_effects=True),
-    )(owners[:, 0], offset_rows, offset_cols, features, w_conv)
+    )
 
     bundle = 4
     span = GROUP * frames_total
@@ -384,14 +475,19 @@
     def fixed(shape):
         return pl.BlockSpec(shape, lambda s: (0,) * len(shape))
 
+    steps = tracks // (GROUP * bundle)
+
+    def block(s):
+        return jnp.minimum(s, steps - 1) // per_block
+
     refined = pl.pallas_call(
-        functools.partial(token_kernel, bundle),
-        grid=(tracks // (GROUP * bundle),),
+        functools.partial(token_kernel, bundle, steps),
+        grid=(steps + 1,),
         out_shape=jax.ShapeDtypeStruct((tracks * frames_total, width), BF16),
         in_specs=[
-            pl.BlockSpec((frames_total, 1, CELLS, chans), lambda s: (0, s // per_block, 0, 0)),
-            pl.BlockSpec((QBLK, chans), lambda s: (s // per_block, 0)),
-            pl.BlockSpec((QBLK,), lambda s: (s // per_block,)),
+            pl.BlockSpec((frames_total, 1, CELLS, chans), lambda s: (0, block(s), 0, 0)),
+            pl.BlockSpec((QBLK, chans), lambda s: (block(s), 0)),
+            pl.BlockSpec((QBLK,), lambda s: (block(s),)),
             fixed(w_corr.shape),
             fixed(w_feat.shape),
             fixed(time_embed.shape),
@@ -402,15 +498,18 @@
             fixed(w_up.shape),
             fixed(w_down.shape),
         ],
-        out_specs=pl.BlockSpec((bundle * span, width), lambda s: (s, 0)),
+        out_specs=pl.BlockSpec((bundle * span, width), lambda s: (jnp.maximum(s - 1, 0), 0)),
         scratch_shapes=[
-            pltpu.VMEM((frames_total, QBLK, width), F32),
+            pltpu.VMEM((width // chans, frames_total * QBLK, chans), F32),
             pltpu.VMEM((2 * chans, width), BF16),
             pltpu.VMEM((3 * width, width), BF16),
+            pltpu.VMEM((2, bundle * span, width), F32),
+            pltpu.VMEM((bundle * span, w_up.shape[1]), BF16),
         ],
+        compiler_params=pltpu.CompilerParams(vmem_limit_bytes=30 * 2**20),
     )(
-        patch, query_feats, start_frames, w_corr, w_feat, time_embed, gain_attn, w_qkv,
-        w_attn_out, gain_mlp, w_up, w_down,
+        patch, query_feats, start_frames, w_corr, w_feat, time_embed, gain_attn, w_qkv, w_attn_out, gain_mlp,
+        w_up, w_down,
     )
     return refined.reshape(tracks, frames_total, width)
 

time: 67.7 us -> 64 us (0.945)
  Pallas kernels: 67.6 us -> 63.7 us
    pallas_call x1, Pallas kernels: 22.8 us -> 20.3 us  [body(): pl.pallas_call(functools.partial(token_kernel, bundle, steps), grid=(step...]
    pallas_call x1, Pallas kernels: 44.8 us -> 43.4 us  [body(): pl.pallas_call(functools.partial(window_kernel, n_tiles, n_frames), out_s...]
where the time goes in v2:
time: 64 us; the launch traced here: 63.9 us
  Pallas kernels  63.7 us (100%)
    pallas_call x1, Pallas kernels, body(): pl.pallas_call(functools.partial(window_kernel, n_tiles, n_frames), out_s...  43.4 us
    pallas_call x1, Pallas kernels, body(): pl.pallas_call(functools.partial(token_kernel, bundle, steps), grid=(step...  20.3 us

profile of v2, /device:TPU:0, one launch (start us, length us, event | category | flops | bytes accessed | tf_op | source)
XLA Modules:
  0.0 63.9 jit_solution(14176715958497152351)
XLA Ops:
  0.0 0.0 copy-start
  0.0 0.0 copy-start.1
  0.0 0.0 copy-start.2
  0.0 0.0 copy-start.3
  0.0 0.0 copy-start.4
  0.0 0.0 copy-start.5
  0.0 0.0 copy-start.6
  0.0 0.0 copy-start.7
  0.0 0.0 copy-start.8
  0.1 0.0 copy-start.9
  0.1 0.0 copy-start.10
  0.1 43.4 %shard_map.154.patch = bf16[16,1,88,128]{3,2,1,0:T(8,128)(2,1)S(1)} custom-call(s32[32]{0:T(128)} %bitcast.2, s32[4,32]{1,0:T(4,128)} %row_in.1, s32[4,32]{1,0:T(4,128)} %col_in.1, bf16[4,8,480,128]{3,2,1,0:T(8,128)(2,1)} %feat.1, bf16[3,3,128,128]{3,2,1,0:T(8,128)(2,1)} %w_conv_in.1), custom_call_target="tpu_custom_call" | custom-call | tf_op jit(solution)/shard_map/pallas_call | solution.py:455
  43.5 0.0 copy-done
  43.5 0.0 copy-done.1
  43.6 0.0 copy-done.2
  43.6 0.0 copy-done.3
  43.6 0.0 copy-done.4
  43.6 0.0 copy-done.5
  43.6 0.0 copy-done.6
  43.6 0.0 copy-done.7
  43.6 0.0 copy-done.8
  43.6 0.0 copy-done.9
  43.6 0.0 copy-done.10
  43.6 20.3 %shard_map.155 = bf16[2048,384]{1,0:T(8,128)(2,1)} custom-call(bf16[16,1,88,128]{3,2,1,0:T(8,128)(2,1)S(1)} %shard_map.154.patch, bf16[128,128]{1,0:T(8,128)(2,1)S(1)} %copy-done.6, s32[128]{0:T(128)S(1)} %copy-done.10, bf16[81,384]{1,0:T(8,128)(2,1)S(1)} %copy-done.5, bf16[128,384]{1,0:T(8,128)(2,1)S(1)} %copy-done.4, f32[16,384]{1,0:T(8,128)S(1)} %copy-done.7, ...), custom_call_target="tpu_custom_call" | custom-call | tf_op jit(solution)/shard_map/pallas_call | solution.py:483
Async XLA Ops:
  0.0 43.5 %copy-start = (bf16[384,1536]{1,0:T(8,128)(2,1)S(1)}, bf16[384,1536]{1,0:T(8,128)(2,1)}, u32[]{:S(2)}) copy-start(bf16[384,1536]{1,0:T(8,128)(2,1)} %w_up.1) | copy-start | bytes 3538948
  0.0 43.5 %copy-start.1 = (bf16[1536,384]{1,0:T(8,128)(2,1)S(1)}, bf16[1536,384]{1,0:T(8,128)(2,1)}, u32[]{:S(2)}) copy-start(bf16[1536,384]{1,0:T(8,128)(2,1)} %w_down.1) | copy-start | bytes 3538948
  0.0 43.5 %copy-start.2 = (bf16[384,1152]{1,0:T(8,128)(2,1)S(1)}, bf16[384,1152]{1,0:T(8,128)(2,1)}, u32[]{:S(2)}) copy-start(bf16[384,1152]{1,0:T(8,128)(2,1)} %w_qkv.1) | copy-start | bytes 2654212
  0.0 43.6 %copy-start.3 = (bf16[384,384]{1,0:T(8,128)(2,1)S(1)}, bf16[384,384]{1,0:T(8,128)(2,1)}, u32[]{:S(2)}) copy-start(bf16[384,384]{1,0:T(8,128)(2,1)} %w_attn_out.1) | copy-start | bytes 884740
  0.0 43.6 %copy-start.4 = (bf16[128,384]{1,0:T(8,128)(2,1)S(1)}, bf16[128,384]{1,0:T(8,128)(2,1)}, u32[]{:S(2)}) copy-start(bf16[128,384]{1,0:T(8,128)(2,1)} %w_feat.1) | copy-start | bytes 294916
  0.0 43.6 %copy-start.5 = (bf16[81,384]{1,0:T(8,128)(2,1)S(1)}, bf16[81,384]{1,0:T(8,128)(2,1)}, u32[]{:S(2)}) copy-start(bf16[81,384]{1,0:T(8,128)(2,1)} %w_corr.1) | copy-start | bytes 186628
  0.0 43.6 %copy-start.6 = (bf16[128,128]{1,0:T(8,128)(2,1)S(1)}, bf16[128,128]{1,0:T(8,128)(2,1)}, u32[]{:S(2)}) copy-start(bf16[128,128]{1,0:T(8,128)(2,1)} %query.1) | copy-start | bytes 98308
  0.0 43.6 %copy-start.7 = (f32[16,384]{1,0:T(8,128)S(1)}, f32[16,384]{1,0:T(8,128)}, u32[]{:S(2)}) copy-start(f32[16,384]{1,0:T(8,128)} %time_embed.1) | copy-start | bytes 73732
  0.0 43.6 %copy-start.8 = (f32[384]{0:T(512)S(1)}, f32[384]{0:T(512)}, u32[]{:S(2)}) copy-start(f32[384]{0:T(512)} %gain_attn.1) | copy-start | bytes 4612
  0.1 43.6 %copy-start.9 = (f32[384]{0:T(512)S(1)}, f32[384]{0:T(512)}, u32[]{:S(2)}) copy-start(f32[384]{0:T(512)} %gain_mlp.1) | copy-start | bytes 4612
  0.1 43.6 %copy-start.10 = (s32[128]{0:T(128)S(1)}, s32[128]{0:T(128)}, u32[]{:S(2)}) copy-start(s32[128]{0:T(128)} %starts.1) | copy-start | bytes 1540

commit v3 on v2

--- a/solution.py
+++ b/solution.py
@@ -20,14 +20,17 @@
 
 
 def window_kernel(
-    n_tiles, n_frames, owners_in, row_in, col_in, feat, w_conv_in, out, owners, row_off, col_off, w_conv, w_cat, padded,
-    conv, win, parts, pairs, sums, lands, total, ready, load_sem, feat_sem, pair_send, pair_recv, hop_send, hop_recv, out_send, out_recv,
+    n_tiles, n_frames, owners_in, row_in, col_in, feat, w_conv_in, query_in, w_corr_in, w_feat_in, time_in, gain_in,
+    w_qkv_in, x_out, qkv_out, owners, row_off, col_off, w_conv, query, w_corr, w_token, time_embed, gain, w_qkv, w_cat,
+    padded, conv, win, parts, pairs, sums, lands, total, ready, windows, load_sem, feat_sem, pair_send, pair_recv,
+    hop_send, hop_recv, out_send, out_recv,
 ):
     tile, group = lax.axis_index("tiles"), lax.axis_index("frames")
     frame_dev, rows, cols, chans = feat.shape
     blocks = owners.shape[0]
     per_group = blocks // n_frames
-    blk_dev = out.shape[1]
+    blk_dev = windows.shape[1]
+    width = gain.shape[0]
     lots = n_frames * blk_dev
     area = WIN * WIN
     chips = n_tiles // 2
@@ -43,7 +46,11 @@
     loads = [
         pltpu.make_async_copy(source, target, load_sem.at[n])
         for n, (source, target) in enumerate(
-            [(w_conv_in, w_conv), (owners_in, owners), (row_in, row_off), (col_in, col_off)]
+            [
+                (w_conv_in, w_conv), (owners_in, owners), (row_in, row_off), (col_in, col_off), (query_in, query),
+                (w_corr_in, w_corr), (w_feat_in, w_token.at[pl.ds(chans, chans)]), (time_in, time_embed),
+                (gain_in, gain), (w_qkv_in, w_qkv),
+            ]
         )
     ]
     fetch(0).start()
@@ -68,7 +75,7 @@
         conv[y] = jnp.zeros(conv.shape[1:], F32)
         conv[WIN + rows + 2 + y] = jnp.zeros(conv.shape[1:], F32)
     conv[WIN : WIN + rows + 2, cols:] = jnp.zeros((rows + 2, conv.shape[1] - cols, chans), F32)
-    for load in loads:
+    for load in loads[:4]:
         load.wait()
     for a in range(3):
         for b in range(3):
@@ -97,7 +104,7 @@
     def handing(step, frame, giver):
         return pltpu.make_async_remote_copy(
             src_ref=ready.at[frame, pl.ds(peers[step][0] * blk_dev, blk_dev)],
-            dst_ref=out.at[giver * frame_dev + frame],
+            dst_ref=windows.at[giver * frame_dev + frame],
             send_sem=out_send.at[step, frame],
             recv_sem=out_recv.at[step, frame],
             device_id=peers[step],
@@ -191,151 +198,155 @@
             ready[frame, lot] = total[lot * area : lot * area + CELLS].astype(BF16)
         for step in range(n_frames - 1):
             handing(step, frame, group).start()
-        out[group * frame_dev + frame] = ready[frame, pl.ds(group * blk_dev, blk_dev)]
-
-    convolve(0)
-    pl.semaphore_wait(barrier, 1 + len(sides) + len(peers))
-
-    def advance(turn, carry):
-        @pl.when((turn > 0) & (turn < frame_dev))
-        def _():
-            convolve(turn)
-
-        @pl.when(turn < frame_dev)
-        def _():
-            cut_all(turn)
-
-            @pl.when(near == 0)
-            def _():
-                move(near_way, turn)
-
-        late = turn - far
-
-        @pl.when((late >= 0) & (late < frame_dev))
-        def _():
-            finish(late)
-            move(far_way, late)
-
-        soon = turn - near
-
-        @pl.when((near > 0) & (soon >= 0) & (soon < frame_dev))
-        def _():
-            move(near_way, soon)
-
-        return carry
-
-    lax.fori_loop(0, frame_dev + chips - 1, advance, 0)
-    for frame in range(frame_dev):
-
-        def drain(dest, carry):
-            pairing(frame, dest).wait_send()
-
-            @pl.when(dest != chip)
-            def _():
-                hop(0, frame, dest).wait_send()
-
-            return carry
-
-        lax.fori_loop(0, chips, drain, 0)
+        windows[group * frame_dev + frame] = ready[frame, pl.ds(group * blk_dev, blk_dev)]
+
+    def project(frame):
         for step in range(n_frames - 1):
-            handing(step, frame, (group + n_frames - step - 1) % n_frames).wait()
-
-
-def rms_scale(values, gain):
-    return values * lax.rsqrt(jnp.mean(values * values, axis=-1, keepdims=True) + 1e-06) * gain
-
-
-def token_kernel(
-    bundle, steps, patch, query, starts, w_corr, w_feat, time_embed, gain_attn, w_qkv, w_attn_out, gain_mlp,
-    w_up, w_down, out, tokens, w_token, w_qkv_t, mixed, hidden,
-):
-    step = pl.program_id(0)
-    frames, _, cells, chans = patch.shape
-    width = w_feat.shape[1]
-    head = width // HEADS
-    span = GROUP * frames
-    per_block = QBLK // (GROUP * bundle)
-    units = w_up.shape[1]
-    lump = 4 * chans
-    down = 2
-
-    @pl.when(step == 0)
-    def _():
-        w_token[:chans] = jnp.zeros((chans, width), BF16)
-        w_token[: w_corr.shape[0]] = w_corr[...]
-        w_token[chans:] = w_feat[...]
-        w_qkv_t[...] = w_qkv[...].T
-
-    @pl.when((step % per_block == 0) & (step < steps))
-    def _():
-        queries = query[...]
-        blank = jnp.zeros((chans - cells, chans), BF16)
-        for some in range(0, frames, 4):
+            handing(step, frame, (group + n_frames - step - 1) % n_frames).wait_recv()
+        at_frames = [giver * frame_dev + frame for giver in range(n_frames)]
+        blank = jnp.zeros((chans - CELLS, chans), BF16)
+        per_blk = QBLK // GROUP
+        for blk in range(blk_dev):
+            queries = query[blk * QBLK : (blk + 1) * QBLK]
             corrs = []
-            for frame in range(some, some + 4):
-                window = jnp.concatenate([patch[frame, 0], blank], axis=0)
+            for at in at_frames:
+                window = jnp.concatenate([windows[at, blk], blank], axis=0)
                 corr = lax.dot_general(
                     queries, window, (((1,), (1,)), ((), ())), preferred_element_type=F32
                 ) * chans ** (-0.5)
                 corrs.append(jnp.concatenate([corr.astype(BF16), queries], axis=1))
             made = jnp.dot(jnp.concatenate(corrs, axis=0), w_token[...], preferred_element_type=F32)
-            for n in range(4):
-                whole = made[n * QBLK : (n + 1) * QBLK] + time_embed[some + n : some + n + 1, :]
-                for plane in range(width // chans):
-                    tokens[plane, pl.ds(some + n, QBLK, stride=frames), :] = whole[
-                        :, plane * chans : (plane + 1) * chans
-                    ]
+            x = jnp.concatenate(
+                [
+                    made[n * QBLK : (n + 1) * QBLK] + time_embed[pl.ds(at, 1), :]
+                    for n, at in enumerate(at_frames)
+                ],
+                axis=0,
+            )
+            normed = rms_scale(x, gain[...]).astype(BF16)
+            qkv = jnp.dot(normed, w_qkv[...], preferred_element_type=F32).astype(BF16)
+            for n, at in enumerate(at_frames):
+                lines = pl.ds(pl.multiple_of(at * GROUP, GROUP), GROUP)
+                held = slice(blk * per_blk, (blk + 1) * per_blk)
+                x_out[held, lines, :] = x[n * QBLK : (n + 1) * QBLK].reshape(per_blk, GROUP, width)
+                qkv_out[held, lines, :] = qkv[n * QBLK : (n + 1) * QBLK].reshape(per_blk, GROUP, 3 * width)
+
+    convolve(0)
+    for load in loads[4:]:
+        load.wait()
+    w_token[:chans] = jnp.zeros((chans, width), BF16)
+    w_token[: w_corr.shape[0]] = w_corr[...]
+    pl.semaphore_wait(barrier, 1 + len(sides) + len(peers))
+
+    def advance(turn, carry):
+        @pl.when((turn > 0) & (turn < frame_dev))
+        def _():
+            convolve(turn)
+
+        @pl.when(turn < frame_dev)
+        def _():
+            cut_all(turn)
+
+            @pl.when(near == 0)
+            def _():
+                move(near_way, turn)
+
+        late = turn - far
+
+        @pl.when((late >= 0) & (late < frame_dev))
+        def _():
+            move(far_way, late)
+
+        @pl.when((late >= 1) & (late <= frame_dev))
+        def _():
+            project(late - 1)
+
+        @pl.when((late >= 0) & (late < frame_dev))
+        def _():
+            finish(late)
+
+        soon = turn - near
+
+        @pl.when((near > 0) & (soon >= 0) & (soon < frame_dev))
+        def _():
+            move(near_way, soon)
+
+        return carry
+
+    lax.fori_loop(0, frame_dev + chips, advance, 0)
+    for frame in range(frame_dev):
+
+        def drain(dest, carry):
+            pairing(frame, dest).wait_send()
+
+            @pl.when(dest != chip)
+            def _():
+                hop(0, frame, dest).wait_send()
+
+            return carry
+
+        lax.fori_loop(0, chips, drain, 0)
+        for step in range(n_frames - 1):
+            handing(step, frame, group).wait_send()
+
+
+def rms_scale(values, gain):
+    return values * lax.rsqrt(jnp.mean(values * values, axis=-1, keepdims=True) + 1e-06) * gain
+
+
+def token_kernel(
+    bundle, steps, tokens, qkv, starts, w_attn_out, gain_mlp, w_up, w_down, out, mixed,
+):
+    step = pl.program_id(0)
+    span, width = tokens.shape[1:]
+    frames = span // GROUP
+    chans = span
+    head = width // HEADS
+    per_block = QBLK // (GROUP * bundle)
+    pieces = 3
 
     key_at = lax.broadcasted_iota(jnp.int32, (span, span), 0)
     query_at = lax.broadcasted_iota(jnp.int32, (span, span), 1)
 
     def attention():
         first = (step % per_block) * (GROUP * bundle)
-        lines = pl.ds(pl.multiple_of(first * frames, span), bundle * span)
-        x = jnp.concatenate([tokens[plane, lines, :] for plane in range(width // chans)], axis=1)
-        normed = rms_scale(x, gain_attn[...]).astype(BF16)
-        qkv = lax.dot_general(
-            w_qkv_t[...], normed, (((1,), (1,)), ((), ())), preferred_element_type=F32
-        ).astype(BF16)
-        same = (key_at // frames) == (query_at // frames)
+        x = tokens[...].reshape(bundle * span, width)
+        same = (key_at % GROUP) == (query_at % GROUP)
         power = head ** (-0.5) * math.log2(math.e)
         start_rows = jnp.broadcast_to(starts[...].astype(F32)[None, :], (GROUP, QBLK)).astype(BF16)
         source = lax.broadcasted_iota(jnp.int32, (QBLK, span), 0)
-        track = lax.broadcasted_iota(jnp.int32, (QBLK, span), 1) // frames
-        nothing = jnp.zeros((head, span), BF16)
+        track = lax.broadcasted_iota(jnp.int32, (QBLK, span), 1) % GROUP
+        lane = lax.broadcasted_iota(jnp.int32, (span, width), 1) // head
+        turned = {}
         yield
         heads, scored, weighed = {}, {}, {}
 
         def score_pair(g, h):
-            at = slice(g * span, (g + 1) * span)
-            one = qkv[h * head : (h + 1) * head, at]
-            two = qkv[(h + 1) * head : (h + 2) * head, at]
+            if h == 0:
+                turned[g] = qkv[g, :, 2 * width :].T
+            low = h * head // chans * chans
+            high = -(-(h + 2) * head // chans) * chans
+            both = qkv[g, :, low:high]
             pair = jnp.concatenate(
-                [jnp.concatenate([one, nothing], axis=1), jnp.concatenate([nothing, two], axis=1)], axis=0
+                [jnp.where(lane[:, low:high] == h + n, both, jnp.zeros_like(both)) for n in range(2)], axis=0
             )
             scored[g, h] = lax.dot_general(
-                qkv[width + h * head : width + (h + 2) * head, at],
-                pair,
-                (((0,), (0,)), ((), ())),
-                preferred_element_type=F32,
+                qkv[g, :, width + low : width + high], pair, (((1,), (1,)), ((), ())), preferred_element_type=F32
             )
 
         def weigh_pair(g, h):
             if h == 0:
                 pick = (source == track + (first + GROUP * g)).astype(BF16)
                 start = jnp.dot(start_rows, pick, preferred_element_type=F32)[:1].astype(jnp.int32)
-                valid = same & ((key_at % frames) >= start)
+                valid = same & ((key_at // GROUP) >= start)
                 masks[g] = jnp.concatenate([valid, valid], axis=1)
             score = jnp.where(masks[g], scored.pop((g, h)), -1e30)
             weight = jnp.exp2((score - jnp.max(score, axis=0, keepdims=True)) * power)
             weighed[g, h] = weight.astype(BF16), jnp.sum(weight, axis=0, keepdims=True)
 
         def value_pair(g, h):
-            at = slice(g * span, (g + 1) * span)
             weight, sums = weighed.pop((g, h))
-            both = jnp.dot(
-                qkv[2 * width + h * head : 2 * width + (h + 2) * head, at], weight, preferred_element_type=F32
-            )
+            both = jnp.dot(turned[g][h * head : (h + 2) * head], weight, preferred_element_type=F32)
             heads[g, h] = (both[:head, :span] / sums[:, :span]).astype(BF16)
             heads[g, h + 1] = (both[head:, span:] / sums[:, span:]).astype(BF16)
 
@@ -359,21 +370,25 @@
         yield
 
     def feed_forward():
+        move = (query_at == (key_at % frames) * GROUP + key_at // frames).astype(BF16)
         base = mixed[(step + 1) % 2]
         normed2 = rms_scale(base, gain_mlp[...]).astype(BF16)
+        units = w_up.shape[1]
+        lump = units // pieces
+        result = base
+        for piece in range(pieces):
+            at = slice(piece * lump, (piece + 1) * lump)
+            raised = jnp.dot(normed2, w_up[:, at], preferred_element_type=F32).astype(BF16)
+            half = raised * 0.5
+            inner = raised * (raised * raised * (0.044715 * math.sqrt(2 / math.pi)) + math.sqrt(2 / math.pi))
+            result = result + jnp.dot(half + half * jnp.tanh(inner), w_down[at, :], preferred_element_type=F32)
+            if piece + 1 < pieces:
+                yield
+        result = result.astype(BF16)
+        for g in range(bundle):
+            at = slice(g * span, (g + 1) * span)
+            out[at, :] = jnp.dot(move, result[at, :], preferred_element_type=F32).astype(BF16)
         yield
-        for at in range(0, units, lump):
-            hidden[:, at : at + lump] = jax.nn.gelu(
-                jnp.dot(normed2, w_up[:, at : at + lump], preferred_element_type=F32), approximate=True
-            ).astype(BF16)
-            yield
-        for part in range(down):
-            stretch = bundle * span // down
-            lines = slice(part * stretch, (part + 1) * stretch)
-            out[lines, :] = (
-                base[lines] + jnp.dot(hidden[lines, :], w_down[...], preferred_element_type=F32)
-            ).astype(BF16)
-            yield
 
     @pl.when(step == 0)
     def _():
@@ -383,16 +398,12 @@
     @pl.when((step > 0) & (step < steps))
     def _():
         ahead, behind = attention(), feed_forward()
-        next(behind)
         next(ahead)
         total = bundle * HEADS // 2
-        parts = units // lump + down
-        done = 0
         for n in range(total):
             next(ahead)
-            while done < parts and (done + 1) * total <= (n + 1) * parts:
+            if n in [total * piece // pieces for piece in range(pieces)]:
                 next(behind)
-                done += 1
         for rest in (ahead, behind):
             for _ in rest:
                 pass
@@ -408,7 +419,7 @@
     for ref in scratch:
         if getattr(ref, "memory_space", None) == pltpu.VMEM:
             held += math.prod(ref.shape) * jnp.dtype(ref.dtype).itemsize
-    return min(held + 6 * 2**20, 58 * 2**20)
+    return min(held + 14 * 2**20, 62 * 2**20)
 
 
 def body(
@@ -433,6 +444,12 @@
         pltpu.SMEM((frame_dev, blocks), jnp.int32),
         pltpu.SMEM((frame_dev, blocks), jnp.int32),
         pltpu.VMEM(w_conv.shape, BF16),
+        pltpu.VMEM(query_feats.shape, BF16),
+        pltpu.VMEM(w_corr.shape, BF16),
+        pltpu.VMEM((2 * chans, width), BF16),
+        pltpu.VMEM(time_embed.shape, F32),
+        pltpu.VMEM(gain_attn.shape, F32),
+        pltpu.VMEM(w_qkv.shape, BF16),
         pltpu.VMEM((3 * chans, 3 * chans), BF16),
         pltpu.VMEM((frame_dev, rows + 4, cols, chans), BF16),
         pltpu.VMEM((rows + 2 + 2 * WIN, cols + 16, chans), F32),
@@ -443,7 +460,8 @@
         pltpu.VMEM((2, frame_dev, chips, span_rows, chans), BF16),
         pltpu.VMEM((total_rows, chans), F32),
         pltpu.VMEM((frame_dev, lots, CELLS, chans), BF16),
-        pltpu.SemaphoreType.DMA((4,)),
+        pltpu.VMEM((frames_total, blk_dev, CELLS, chans), BF16),
+        pltpu.SemaphoreType.DMA((10,)),
         pltpu.SemaphoreType.DMA((frame_dev,)),
         pltpu.SemaphoreType.DMA((frame_dev, chips)),
         pltpu.SemaphoreType.DMA((frame_dev, chips)),
@@ -452,47 +470,44 @@
         pltpu.SemaphoreType.DMA((n_frames - 1, frame_dev)),
         pltpu.SemaphoreType.DMA((n_frames - 1, frame_dev)),
     ]
-    patch = pl.pallas_call(
+    tracks = blk_dev * QBLK
+    span = GROUP * frames_total
+    groups = tracks // GROUP
+    given = (
+        owners[:, 0], offset_rows, offset_cols, features, w_conv, query_feats, w_corr, w_feat, time_embed, gain_attn, w_qkv,
+    )
+    tokens, qkv = pl.pallas_call(
         functools.partial(window_kernel, n_tiles, n_frames),
-        out_shape=jax.ShapeDtypeStruct((frames_total, blk_dev, CELLS, chans), BF16),
-        in_specs=[pl.BlockSpec(memory_space=pltpu.HBM)] * 5,
-        out_specs=whole,
+        out_shape=[
+            jax.ShapeDtypeStruct((groups, span, width), F32),
+            jax.ShapeDtypeStruct((groups, span, 3 * width), BF16),
+        ],
+        in_specs=[pl.BlockSpec(memory_space=pltpu.HBM)] * len(given),
+        out_specs=[whole, whole],
         scratch_shapes=scratch,
         compiler_params=pltpu.CompilerParams(
             collective_id=0, has_side_effects=True, vmem_limit_bytes=grant(scratch)
         ),
-    )(
-        *[
-            pltpu.with_memory_space_constraint(x, pltpu.HBM)
-            for x in (owners[:, 0], offset_rows, offset_cols, features, w_conv)
-        ]
-    )
+    )(*[pltpu.with_memory_space_constraint(x, pltpu.HBM) for x in given])
 
     bundle = 4
-    span = GROUP * frames_total
-    tracks = blk_dev * QBLK
     per_block = QBLK // (GROUP * bundle)
+    steps = groups // bundle
+
     def fixed(shape):
         return pl.BlockSpec(shape, lambda s: (0,) * len(shape))
 
-    steps = tracks // (GROUP * bundle)
-
-    def block(s):
-        return jnp.minimum(s, steps - 1) // per_block
+    def ahead(s):
+        return jnp.minimum(s, steps - 1)
 
     refined = pl.pallas_call(
         functools.partial(token_kernel, bundle, steps),
         grid=(steps + 1,),
         out_shape=jax.ShapeDtypeStruct((tracks * frames_total, width), BF16),
         in_specs=[
-            pl.BlockSpec((frames_total, 1, CELLS, chans), lambda s: (0, block(s), 0, 0)),
-            pl.BlockSpec((QBLK, chans), lambda s: (block(s), 0)),
-            pl.BlockSpec((QBLK,), lambda s: (block(s),)),
-            fixed(w_corr.shape),
-            fixed(w_feat.shape),
-            fixed(time_embed.shape),
-            fixed((width,)),
-            fixed(w_qkv.shape),
+            pl.BlockSpec((bundle, span, width), lambda s: (ahead(s), 0, 0)),
+            pl.BlockSpec((bundle, span, 3 * width), lambda s: (ahead(s), 0, 0)),
+            pl.BlockSpec((QBLK,), lambda s: (ahead(s) // per_block,)),
             fixed(w_attn_out.shape),
             fixed((width,)),
             fixed(w_up.shape),
@@ -500,17 +515,10 @@
         ],
         out_specs=pl.BlockSpec((bundle * span, width), lambda s: (jnp.maximum(s - 1, 0), 0)),
         scratch_shapes=[
-            pltpu.VMEM((width // chans, frames_total * QBLK, chans), F32),
-            pltpu.VMEM((2 * chans, width), BF16),
-            pltpu.VMEM((3 * width, width), BF16),
             pltpu.VMEM((2, bundle * span, width), F32),
-            pltpu.VMEM((bundle * span, w_up.shape[1]), BF16),
         ],
-        compiler_params=pltpu.CompilerParams(vmem_limit_bytes=30 * 2**20),
-    )(
-        patch, query_feats, start_frames, w_corr, w_feat, time_embed, gain_attn, w_qkv, w_attn_out, gain_mlp,
-        w_up, w_down,
-    )
+        compiler_params=pltpu.CompilerParams(vmem_limit_bytes=28 * 2**20),
+    )(tokens, qkv, start_frames, w_attn_out, gain_mlp, w_up, w_down)
     return refined.reshape(tracks, frames_total, width)
 
 

time: 64 us -> 59.2 us (0.925)
  Pallas kernels: 63.7 us -> 59 us
    pallas_call x1, Pallas kernels: 20.3 us -> 15.1 us  [body(): pl.pallas_call(functools.partial(token_kernel, bundle, steps), grid=(step...]
where the time goes in v3:
time: 59.2 us; the launch traced here: 59.1 us
  Pallas kernels  59 us (100%)
    pallas_call x1, Pallas kernels, body(): pl.pallas_call(functools.partial(window_kernel, n_tiles, n_frames), out_s...  43.9 us
    pallas_call x1, Pallas kernels, body(): pl.pallas_call(functools.partial(token_kernel, bundle, steps), grid=(step...  15.1 us

profile of v3, /device:TPU:0, one launch (start us, length us, event | category | flops | bytes accessed | tf_op | source)
XLA Modules:
  0.0 59.1 jit_solution(15918560397172035539)
XLA Ops:
  0.0 0.0 copy-start.1
  0.0 0.0 copy-start
  0.0 0.0 copy-start.3
  0.0 0.0 copy-start.2
  0.0 0.0 copy-start.4
  0.0 43.9 %shard_map.154 = (f32[16,128,384]{2,1,0:T(8,128)S(1)}, bf16[16,128,1152]{2,1,0:T(8,128)(2,1)S(1)}) custom-call(s32[32]{0:T(128)} %bitcast.2, s32[4,32]{1,0:T(4,128)} %row_in.1, s32[4,32]{1,0:T(4,128)} %col_in.1, bf16[4,8,480,128]{3,2,1,0:T(8,128)(2,1)} %feat.1, bf16[3,3,128,128]{3,2,1,0:T(8,128)(2,1)} %w_conv_in.1, bf16[128,128]{1,0:T(8,128)(2,1)} %query_in.1, ...), custom_call_target="tpu_custom_call" | custom-call | tf_op jit(solution)/shard_map/pallas_call | solution.py:479
  43.9 0.0 copy-done.1
  43.9 0.0 copy-done
  43.9 0.0 copy-done.3
  43.9 0.0 copy-done.2
  43.9 0.0 copy-done.4
  43.9 15.1 %shard_map.155 = bf16[2048,384]{1,0:T(8,128)(2,1)} custom-call(f32[16,128,384]{2,1,0:T(8,128)S(1)} %get-tuple-element.7.tokens, bf16[16,128,1152]{2,1,0:T(8,128)(2,1)S(1)} %get-tuple-element.8.qkv, s32[128]{0:T(128)S(1)} %copy-done.4, bf16[384,384]{1,0:T(8,128)(2,1)S(1)} %copy-done.2, f32[384]{0:T(512)S(1)} %copy-done.3, bf16[384,1536]{1,0:T(8,128)(2,1)S(1)} %copy-done, ...), custom_call_target="tpu_custom_call" | custom-call | tf_op jit(solution)/shard_map/pallas_call | solution.py:503
Async XLA Ops:
  0.0 43.9 %copy-start.1 = (bf16[1536,384]{1,0:T(8,128)(2,1)S(1)}, bf16[1536,384]{1,0:T(8,128)(2,1)}, u32[]{:S(2)}) copy-start(bf16[1536,384]{1,0:T(8,128)(2,1)} %w_down.1) | copy-start | bytes 3538948
  0.0 43.9 %copy-start = (bf16[384,1536]{1,0:T(8,128)(2,1)S(1)}, bf16[384,1536]{1,0:T(8,128)(2,1)}, u32[]{:S(2)}) copy-start(bf16[384,1536]{1,0:T(8,128)(2,1)} %w_up.1) | copy-start | bytes 3538948
  0.0 43.9 %copy-start.3 = (f32[384]{0:T(512)S(1)}, f32[384]{0:T(512)}, u32[]{:S(2)}) copy-start(f32[384]{0:T(512)} %gain_mlp.1) | copy-start | bytes 4612
  0.0 43.9 %copy-start.2 = (bf16[384,384]{1,0:T(8,128)(2,1)S(1)}, bf16[384,384]{1,0:T(8,128)(2,1)}, u32[]{:S(2)}) copy-start(bf16[384,384]{1,0:T(8,128)(2,1)} %w_attn_out.1) | copy-start | bytes 884740
  0.0 43.9 %copy-start.4 = (s32[128]{0:T(128)S(1)}, s32[128]{0:T(128)}, u32[]{:S(2)}) copy-start(s32[128]{0:T(128)} %starts.1) | copy-start | bytes 1540

commit v4 on v3

--- a/solution.py
+++ b/solution.py
@@ -77,9 +77,13 @@
     conv[WIN : WIN + rows + 2, cols:] = jnp.zeros((rows + 2, conv.shape[1] - cols, chans), F32)
     for load in loads[:4]:
         load.wait()
-    for a in range(3):
+    for half in range(2):
         for b in range(3):
-            w_cat[a * chans : (a + 1) * chans, b * chans : (b + 1) * chans] = w_conv[a, b]
+            at = (3 * half + b) * chans
+            spare = 3 * (1 - half) * chans
+            w_cat[spare : spare + chans, at : at + chans] = jnp.zeros((chans, chans), BF16)
+            for a in range(3):
+                w_cat[(half + a) * chans : (half + a + 1) * chans, at : at + chans] = w_conv[a, b]
 
     def pairing(frame, dest):
         return pltpu.make_async_remote_copy(
@@ -115,17 +119,18 @@
         fetch(frame).wait()
 
         def conv_rows(pair, carry):
+            y = 2 * pair
+            wide = jnp.concatenate([padded[frame, y + n] for n in range(4)], axis=-1)
+            made = jnp.dot(wide, w_cat[...], preferred_element_type=F32)
+            edge = jnp.zeros((1, chans), F32)
             for half in range(2):
-                y = 2 * pair + half
-                wide = jnp.concatenate([padded[frame, y], padded[frame, y + 1], padded[frame, y + 2]], axis=-1)
-                sums_at = jnp.dot(wide, w_cat[...], preferred_element_type=F32)
-                edge = jnp.zeros((1, chans), F32)
-                left = jnp.concatenate([edge, sums_at[: cols - 1, :chans]], axis=0)
-                right = jnp.concatenate([sums_at[1:, 2 * chans :], edge], axis=0)
-                conv[WIN + y, :cols] = left + sums_at[:, chans : 2 * chans] + right
+                at = 3 * half * chans
+                left = jnp.concatenate([edge, made[: cols - 1, at : at + chans]], axis=0)
+                right = jnp.concatenate([made[1:, at + 2 * chans : at + 3 * chans], edge], axis=0)
+                conv[WIN + y + half, :cols] = left + made[:, at + chans : at + 2 * chans] + right
             return carry
 
-        lax.fori_loop(0, (rows + 2) // 2, conv_rows, 0)
+        lax.fori_loop(0, (rows + 2) // 2, conv_rows, 0, unroll=True)
 
         @pl.when(tile == 0)
         def _():
@@ -224,7 +229,9 @@
                 axis=0,
             )
             normed = rms_scale(x, gain[...]).astype(BF16)
-            qkv = jnp.dot(normed, w_qkv[...], preferred_element_type=F32).astype(BF16)
+            made = jnp.dot(normed, w_qkv[...], preferred_element_type=F32)
+            power = (width // HEADS) ** (-0.5) * math.log2(math.e)
+            qkv = jnp.concatenate([(made[:, :width] * power).astype(BF16), made[:, width:].astype(BF16)], axis=1)
             for n, at in enumerate(at_frames):
                 lines = pl.ds(pl.multiple_of(at * GROUP, GROUP), GROUP)
                 held = slice(blk * per_blk, (blk + 1) * per_blk)
@@ -312,7 +319,7 @@
         first = (step % per_block) * (GROUP * bundle)
         x = tokens[...].reshape(bundle * span, width)
         same = (key_at % GROUP) == (query_at % GROUP)
-        power = head ** (-0.5) * math.log2(math.e)
+        ones = jnp.ones((2 * GROUP, span), BF16)
         start_rows = jnp.broadcast_to(starts[...].astype(F32)[None, :], (GROUP, QBLK)).astype(BF16)
         source = lax.broadcasted_iota(jnp.int32, (QBLK, span), 0)
         track = lax.broadcasted_iota(jnp.int32, (QBLK, span), 1) % GROUP
@@ -341,18 +348,18 @@
                 valid = same & ((key_at // GROUP) >= start)
                 masks[g] = jnp.concatenate([valid, valid], axis=1)
             score = jnp.where(masks[g], scored.pop((g, h)), -1e30)
-            weight = jnp.exp2((score - jnp.max(score, axis=0, keepdims=True)) * power)
-            weighed[g, h] = weight.astype(BF16), jnp.sum(weight, axis=0, keepdims=True)
+            weighed[g, h] = jnp.exp2((score - jnp.max(score, axis=0, keepdims=True)).astype(BF16))
 
         def value_pair(g, h):
-            weight, sums = weighed.pop((g, h))
-            both = jnp.dot(turned[g][h * head : (h + 2) * head], weight, preferred_element_type=F32)
-            heads[g, h] = (both[:head, :span] / sums[:, :span]).astype(BF16)
-            heads[g, h + 1] = (both[head:, span:] / sums[:, span:]).astype(BF16)
+            lines = jnp.concatenate([turned[g][h * head : (h + 2) * head], ones], axis=0)
+            both = jnp.dot(lines, weighed.pop((g, h)), preferred_element_type=F32)
+            sums = 1.0 / both[2 * head : 2 * head + 1]
+            heads[g, h] = (both[:head, :span] * sums[:, :span]).astype(BF16)
+            heads[g, h + 1] = (both[head : 2 * head, span:] * sums[:, span:]).astype(BF16)
 
         masks = {}
         pairs = [(g, h) for g in range(bundle) for h in range(0, HEADS, 2)]
-        lead = 2
+        lead = 4
         for n in range(len(pairs) + 2 * lead):
             if n < len(pairs):
                 score_pair(*pairs[n])
@@ -450,7 +457,7 @@
         pltpu.VMEM(time_embed.shape, F32),
         pltpu.VMEM(gain_attn.shape, F32),
         pltpu.VMEM(w_qkv.shape, BF16),
-        pltpu.VMEM((3 * chans, 3 * chans), BF16),
+        pltpu.VMEM((4 * chans, 6 * chans), BF16),
         pltpu.VMEM((frame_dev, rows + 4, cols, chans), BF16),
         pltpu.VMEM((rows + 2 + 2 * WIN, cols + 16, chans), F32),
         pltpu.VMEM((2, span_rows, chans), F32),

time: 59.2 us -> 57 us (0.963)
  Pallas kernels: 59 us -> 56.8 us
    pallas_call x1, Pallas kernels: 43.9 us -> 42.3 us  [body(): pl.pallas_call(functools.partial(window_kernel, n_tiles, n_frames), out_s...]
    pallas_call x1, Pallas kernels: 15.1 us -> 14.5 us  [body(): pl.pallas_call(functools.partial(token_kernel, bundle, steps), grid=(step...]
where the time goes in v4:
time: 57 us; the launch traced here: 56.8 us
  Pallas kernels  56.8 us (100%)
    pallas_call x1, Pallas kernels, body(): pl.pallas_call(functools.partial(window_kernel, n_tiles, n_frames), out_s...  42.3 us
    pallas_call x1, Pallas kernels, body(): pl.pallas_call(functools.partial(token_kernel, bundle, steps), grid=(step...  14.5 us

profile of v4, /device:TPU:0, one launch (start us, length us, event | category | flops | bytes accessed | tf_op | source)
XLA Modules:
  0.0 56.8 jit_solution(15727412056721132350)
XLA Ops:
  0.0 0.0 copy-start.1
  0.0 0.0 copy-start
  0.0 0.0 copy-start.3
  0.0 0.0 copy-start.2
  0.0 0.0 copy-start.4
  0.0 42.3 %shard_map.154 = (f32[16,128,384]{2,1,0:T(8,128)S(1)}, bf16[16,128,1152]{2,1,0:T(8,128)(2,1)S(1)}) custom-call(s32[32]{0:T(128)} %bitcast.2, s32[4,32]{1,0:T(4,128)} %row_in.1, s32[4,32]{1,0:T(4,128)} %col_in.1, bf16[4,8,480,128]{3,2,1,0:T(8,128)(2,1)} %feat.1, bf16[3,3,128,128]{3,2,1,0:T(8,128)(2,1)} %w_conv_in.1, bf16[128,128]{1,0:T(8,128)(2,1)} %query_in.1, ...), custom_call_target="tpu_custom_call" | custom-call | tf_op jit(solution)/shard_map/pallas_call | solution.py:486
  42.3 0.0 copy-done.1
  42.3 0.0 copy-done
  42.3 0.0 copy-done.3
  42.3 0.0 copy-done.2
  42.4 0.0 copy-done.4
  42.4 14.5 %shard_map.155 = bf16[2048,384]{1,0:T(8,128)(2,1)} custom-call(f32[16,128,384]{2,1,0:T(8,128)S(1)} %get-tuple-element.7.tokens, bf16[16,128,1152]{2,1,0:T(8,128)(2,1)S(1)} %get-tuple-element.8.qkv, s32[128]{0:T(128)S(1)} %copy-done.4, bf16[384,384]{1,0:T(8,128)(2,1)S(1)} %copy-done.2, f32[384]{0:T(512)S(1)} %copy-done.3, bf16[384,1536]{1,0:T(8,128)(2,1)S(1)} %copy-done, ...), custom_call_target="tpu_custom_call" | custom-call | tf_op jit(solution)/shard_map/pallas_call | solution.py:510
Async XLA Ops:
  0.0 42.3 %copy-start.1 = (bf16[1536,384]{1,0:T(8,128)(2,1)S(1)}, bf16[1536,384]{1,0:T(8,128)(2,1)}, u32[]{:S(2)}) copy-start(bf16[1536,384]{1,0:T(8,128)(2,1)} %w_down.1) | copy-start | bytes 3538948
  0.0 42.3 %copy-start = (bf16[384,1536]{1,0:T(8,128)(2,1)S(1)}, bf16[384,1536]{1,0:T(8,128)(2,1)}, u32[]{:S(2)}) copy-start(bf16[384,1536]{1,0:T(8,128)(2,1)} %w_up.1) | copy-start | bytes 3538948
  0.0 42.3 %copy-start.3 = (f32[384]{0:T(512)S(1)}, f32[384]{0:T(512)}, u32[]{:S(2)}) copy-start(f32[384]{0:T(512)} %gain_mlp.1) | copy-start | bytes 4612
  0.0 42.3 %copy-start.2 = (bf16[384,384]{1,0:T(8,128)(2,1)S(1)}, bf16[384,384]{1,0:T(8,128)(2,1)}, u32[]{:S(2)}) copy-start(bf16[384,384]{1,0:T(8,128)(2,1)} %w_attn_out.1) | copy-start | bytes 884740
  0.0 42.4 %copy-start.4 = (s32[128]{0:T(128)S(1)}, s32[128]{0:T(128)}, u32[]{:S(2)}) copy-start(s32[128]{0:T(128)} %starts.1) | copy-start | bytes 1540

commit v5 on v4

--- a/solution.py
+++ b/solution.py
@@ -359,7 +359,7 @@
 
         masks = {}
         pairs = [(g, h) for g in range(bundle) for h in range(0, HEADS, 2)]
-        lead = 4
+        lead = 6
         for n in range(len(pairs) + 2 * lead):
             if n < len(pairs):
                 score_pair(*pairs[n])
@@ -497,7 +497,7 @@
         ),
     )(*[pltpu.with_memory_space_constraint(x, pltpu.HBM) for x in given])
 
-    bundle = 4
+    bundle = 8
     per_block = QBLK // (GROUP * bundle)
     steps = groups // bundle
 
@@ -524,7 +524,7 @@
         scratch_shapes=[
             pltpu.VMEM((2, bundle * span, width), F32),
         ],
-        compiler_params=pltpu.CompilerParams(vmem_limit_bytes=28 * 2**20),
+        compiler_params=pltpu.CompilerParams(vmem_limit_bytes=36 * 2**20),
     )(tokens, qkv, start_frames, w_attn_out, gain_mlp, w_up, w_down)
     return refined.reshape(tracks, frames_total, width)
 

time: 57 us -> 56.3 us (0.988)
  Pallas kernels: 56.8 us -> 56 us
    pallas_call x1, Pallas kernels: 14.5 us -> 13.8 us  [body(): pl.pallas_call(functools.partial(token_kernel, bundle, steps), grid=(step...]
where the time goes in v5:
time: 56.3 us; the launch traced here: 56.1 us
  Pallas kernels  56 us (99%)
    pallas_call x1, Pallas kernels, body(): pl.pallas_call(functools.partial(window_kernel, n_tiles, n_frames), out_s...  42.3 us
    pallas_call x1, Pallas kernels, body(): pl.pallas_call(functools.partial(token_kernel, bundle, steps), grid=(step...  13.8 us

profile of v5, /device:TPU:0, one launch (start us, length us, event | category | flops | bytes accessed | tf_op | source)
XLA Modules:
  0.0 56.1 jit_solution(10336926585188926861)
XLA Ops:
  0.0 0.0 copy-start.1
  0.0 0.0 copy-start
  0.0 0.0 copy-start.3
  0.0 0.0 copy-start.2
  0.0 0.0 copy-start.4
  0.0 42.3 %shard_map.154 = (f32[16,128,384]{2,1,0:T(8,128)S(1)}, bf16[16,128,1152]{2,1,0:T(8,128)(2,1)S(1)}) custom-call(s32[32]{0:T(128)} %bitcast.2, s32[4,32]{1,0:T(4,128)} %row_in.1, s32[4,32]{1,0:T(4,128)} %col_in.1, bf16[4,8,480,128]{3,2,1,0:T(8,128)(2,1)} %feat.1, bf16[3,3,128,128]{3,2,1,0:T(8,128)(2,1)} %w_conv_in.1, bf16[128,128]{1,0:T(8,128)(2,1)} %query_in.1, ...), custom_call_target="tpu_custom_call" | custom-call | tf_op jit(solution)/shard_map/pallas_call | solution.py:486
  42.3 0.0 copy-done.1
  42.3 0.0 copy-done
  42.3 0.0 copy-done.3
  42.3 0.0 copy-done.2
  42.4 0.0 copy-done.4
  42.4 13.8 %shard_map.155 = bf16[2048,384]{1,0:T(8,128)(2,1)} custom-call(f32[16,128,384]{2,1,0:T(8,128)S(1)} %get-tuple-element.7.tokens, bf16[16,128,1152]{2,1,0:T(8,128)(2,1)S(1)} %get-tuple-element.8.qkv, s32[128]{0:T(128)S(1)} %copy-done.4, bf16[384,384]{1,0:T(8,128)(2,1)S(1)} %copy-done.2, f32[384]{0:T(512)S(1)} %copy-done.3, bf16[384,1536]{1,0:T(8,128)(2,1)S(1)} %copy-done, ...), custom_call_target="tpu_custom_call" | custom-call | tf_op jit(solution)/shard_map/pallas_call | solution.py:510
Async XLA Ops:
  0.0 42.3 %copy-start.1 = (bf16[1536,384]{1,0:T(8,128)(2,1)S(1)}, bf16[1536,384]{1,0:T(8,128)(2,1)}, u32[]{:S(2)}) copy-start(bf16[1536,384]{1,0:T(8,128)(2,1)} %w_down.1) | copy-start | bytes 3538948
  0.0 42.3 %copy-start = (bf16[384,1536]{1,0:T(8,128)(2,1)S(1)}, bf16[384,1536]{1,0:T(8,128)(2,1)}, u32[]{:S(2)}) copy-start(bf16[384,1536]{1,0:T(8,128)(2,1)} %w_up.1) | copy-start | bytes 3538948
  0.0 42.3 %copy-start.3 = (f32[384]{0:T(512)S(1)}, f32[384]{0:T(512)}, u32[]{:S(2)}) copy-start(f32[384]{0:T(512)} %gain_mlp.1) | copy-start | bytes 4612
  0.0 42.3 %copy-start.2 = (bf16[384,384]{1,0:T(8,128)(2,1)S(1)}, bf16[384,384]{1,0:T(8,128)(2,1)}, u32[]{:S(2)}) copy-start(bf16[384,384]{1,0:T(8,128)(2,1)} %w_attn_out.1) | copy-start | bytes 884740
  0.0 42.3 %copy-start.4 = (s32[128]{0:T(128)S(1)}, s32[128]{0:T(128)}, u32[]{:S(2)}) copy-start(s32[128]{0:T(128)} %starts.1) | copy-start | bytes 1540

commit v6 on v5

--- a/solution.py
+++ b/solution.py
@@ -409,7 +409,7 @@
         total = bundle * HEADS // 2
         for n in range(total):
             next(ahead)
-            if n in [total * piece // pieces for piece in range(pieces)]:
+            if n in [total * (2 * piece + 1) // (2 * pieces) for piece in range(pieces)]:
                 next(behind)
         for rest in (ahead, behind):
             for _ in rest:

time: 56.3 us -> 56.1 us (level)
  no operation moved by 1% of the time
where the time goes in v6:
time: 56.1 us; the launch traced here: 56 us
  Pallas kernels  55.9 us (100%)
    pallas_call x1, Pallas kernels, body(): pl.pallas_call(functools.partial(window_kernel, n_tiles, n_frames), out_s...  42.3 us
    pallas_call x1, Pallas kernels, body(): pl.pallas_call(functools.partial(token_kernel, bundle, steps), grid=(step...  13.6 us

profile of v6, /device:TPU:0, one launch (start us, length us, event | category | flops | bytes accessed | tf_op | source)
XLA Modules:
  0.0 56.0 jit_solution(12358980358377751059)
XLA Ops:
  0.0 0.0 copy-start.1
  0.0 0.0 copy-start
  0.0 0.0 copy-start.3
  0.0 0.0 copy-start.2
  0.0 0.0 copy-start.4
  0.0 42.3 %shard_map.154 = (f32[16,128,384]{2,1,0:T(8,128)S(1)}, bf16[16,128,1152]{2,1,0:T(8,128)(2,1)S(1)}) custom-call(s32[32]{0:T(128)} %bitcast.2, s32[4,32]{1,0:T(4,128)} %row_in.1, s32[4,32]{1,0:T(4,128)} %col_in.1, bf16[4,8,480,128]{3,2,1,0:T(8,128)(2,1)} %feat.1, bf16[3,3,128,128]{3,2,1,0:T(8,128)(2,1)} %w_conv_in.1, bf16[128,128]{1,0:T(8,128)(2,1)} %query_in.1, ...), custom_call_target="tpu_custom_call" | custom-call | tf_op jit(solution)/shard_map/pallas_call | solution.py:486
  42.3 0.0 copy-done.1
  42.3 0.0 copy-done
  42.3 0.0 copy-done.3
  42.3 0.0 copy-done.2
  42.4 0.0 copy-done.4
  42.4 13.6 %shard_map.155 = bf16[2048,384]{1,0:T(8,128)(2,1)} custom-call(f32[16,128,384]{2,1,0:T(8,128)S(1)} %get-tuple-element.7.tokens, bf16[16,128,1152]{2,1,0:T(8,128)(2,1)S(1)} %get-tuple-element.8.qkv, s32[128]{0:T(128)S(1)} %copy-done.4, bf16[384,384]{1,0:T(8,128)(2,1)S(1)} %copy-done.2, f32[384]{0:T(512)S(1)} %copy-done.3, bf16[384,1536]{1,0:T(8,128)(2,1)S(1)} %copy-done, ...), custom_call_target="tpu_custom_call" | custom-call | tf_op jit(solution)/shard_map/pallas_call | solution.py:510
Async XLA Ops:
  0.0 42.3 %copy-start.1 = (bf16[1536,384]{1,0:T(8,128)(2,1)S(1)}, bf16[1536,384]{1,0:T(8,128)(2,1)}, u32[]{:S(2)}) copy-start(bf16[1536,384]{1,0:T(8,128)(2,1)} %w_down.1) | copy-start | bytes 3538948
  0.0 42.3 %copy-start = (bf16[384,1536]{1,0:T(8,128)(2,1)S(1)}, bf16[384,1536]{1,0:T(8,128)(2,1)}, u32[]{:S(2)}) copy-start(bf16[384,1536]{1,0:T(8,128)(2,1)} %w_up.1) | copy-start | bytes 3538948
  0.0 42.3 %copy-start.3 = (f32[384]{0:T(512)S(1)}, f32[384]{0:T(512)}, u32[]{:S(2)}) copy-start(f32[384]{0:T(512)} %gain_mlp.1) | copy-start | bytes 4612
  0.0 42.3 %copy-start.2 = (bf16[384,384]{1,0:T(8,128)(2,1)S(1)}, bf16[384,384]{1,0:T(8,128)(2,1)}, u32[]{:S(2)}) copy-start(bf16[384,384]{1,0:T(8,128)(2,1)} %w_attn_out.1) | copy-start | bytes 884740
  0.0 42.3 %copy-start.4 = (s32[128]{0:T(128)S(1)}, s32[128]{0:T(128)}, u32[]{:S(2)}) copy-start(s32[128]{0:T(128)} %starts.1) | copy-start | bytes 1540
